TPU v7x, 32 devices: a whole 2x2x4 slice. The times are simulated.
32 devices in a mesh: parts: 2 (over y), ep: 16 (over z, x, core).
Axes of the slice: x: 2, y: 2, z: 4, core: 2. Of those that a mesh axis runs over, the one named last changes fastest.
Arguments:
- tokens: bfloat16 [512, 2048], P(('parts', 'ep')), parts along dimension 0, may hold values from -6 to 6
- gate_up: bfloat16 [4096, 16, 1536], P(('parts', 'ep')), parts along dimension 0, may hold values from -0.125 to 0.125
- down_proj: bfloat16 [1536, 16, 2048], P(('parts', 'ep')), parts along dimension 0, may hold values from -0.21875 to 0.21875
- expert_ids: int32 [512, 8], P(('parts', 'ep')), parts along dimension 0, may hold values from 0 to 15, all different within a row; in each aligned block of 16 rows (0 to 15, 16 to 31, ...) at most 16 rows name the same one
- gate_weights: float32 [512, 8], P(('parts', 'ep')), parts along dimension 0, may hold values from 0.03 to 0.6
- owner_slot: int32 [32], P('parts'), parts along dimension 0, may hold values from 0 to 15, each once
Outputs:
- moe_out: bfloat16 [512, 2048], P(('parts', 'ep')), parts along dimension 0
- channel_scale: float32 [32, 3584], P(('parts', 'ep')), parts along dimension 0
There are 2 independent parts, one for each index of `parts`. A program takes and returns all parts, laid end to end along the dimension named above; each array names one. Nothing has to cross between parts.
Inputs may be any that keep to these rules, and one draw needn't show every extreme that they name: `expert_ids`: each row names 8 different experts; among the rows of one device no expert is named more than 16 times, a bound that some block reaches. `owner_slot`: A permutation: each slot holds exactly one expert.
All inputs are finite; a program needn't handle non-finite values.
Results may differ from a plain program's by a relative error of at most 0.0058.
Values may be sent and summed in bfloat16 or wider, within the bound.
No kernel may reach another device: no remote copies, remote signals or barrier semaphores. Data moves between devices by JAX's collectives and lax.ppermute only.
A program may use at most 128 MiB of HBM per device.

v0:
```python
import math

import jax
import jax.numpy as jnp
from jax import lax
from jax.sharding import PartitionSpec as P


def expert_block(arrived, held_up, held_down):
    hidden = jnp.einsum("rjd,djf->rjf", arrived, held_up, preferred_element_type=jnp.float32)
    ffn_width = held_up.shape[2] // 2
    activated = (jax.nn.silu(hidden[..., :ffn_width]) * hidden[..., ffn_width:]).astype(
        jnp.bfloat16
    )
    return jnp.einsum(
        "rjf,fjd->rjd", activated, held_down, preferred_element_type=jnp.float32
    ).astype(jnp.bfloat16)


def column_scales(gate_up, down_proj):
    gate_scale = jnp.max(jnp.abs(gate_up), axis=0).astype(jnp.float32) * math.sqrt(gate_up.shape[0])
    down_scale = jnp.max(jnp.abs(down_proj), axis=0).astype(jnp.float32) * math.sqrt(
        down_proj.shape[0]
    )
    return jnp.concatenate([gate_scale, down_scale], axis=1)


def shards(tokens, gate_up, down_proj, expert_ids, gate_weights, owner_slot):
    tok_rows, model_width = tokens.shape
    top_count = expert_ids.shape[1]
    slots_all = gate_up.shape[1]
    devices = lax.axis_size("ep")
    own_count = slots_all // devices
    capacity = 2 * tok_rows * top_count // slots_all
    experts_iota = jnp.arange(slots_all, dtype=jnp.int32)
    inverse = jnp.zeros((slots_all,), jnp.int32).at[owner_slot].set(experts_iota)
    flat_ids = expert_ids.reshape(-1)
    one_hot = (flat_ids[:, None] == experts_iota[None, :]).astype(jnp.int32)
    slot_rank = jnp.sum((jnp.cumsum(one_hot, axis=0) - 1) * one_hot, axis=1)
    position = slot_rank * slots_all + flat_ids
    source_rows = jnp.repeat(tokens, top_count, axis=0)
    outbox = (
        jnp.zeros((capacity * slots_all, model_width), jnp.bfloat16).at[position].set(source_rows)
    )
    outbox = outbox.reshape(capacity, slots_all, model_width)
    held_up, held_down = (
        lax.all_to_all(gate_up, "ep", split_axis=1, concat_axis=0, tiled=True),
        lax.all_to_all(down_proj, "ep", split_axis=1, concat_axis=0, tiled=True),
    )
    arrived = lax.all_to_all(outbox, "ep", split_axis=1, concat_axis=0, tiled=True)
    expert_out = expert_block(arrived, held_up, held_down)
    returned = lax.all_to_all(expert_out, "ep", split_axis=0, concat_axis=1, tiled=True).reshape(
        capacity * slots_all, model_width
    )
    picked = returned[position].astype(jnp.float32).reshape(tok_rows, top_count, model_width)
    moe_out = jnp.sum(picked * gate_weights[:, :, None], axis=1).astype(jnp.bfloat16)
    scales = column_scales(held_up, held_down)
    every_row = lax.all_gather(scales, "ep", axis=0, tiled=True)
    mine = lax.dynamic_slice_in_dim(inverse, lax.axis_index("ep") * own_count, own_count)
    scales = jnp.take(every_row, mine, axis=0)
    return (moe_out, scales)


def solution(mesh):
    in_specs = (
        P(("parts", "ep"), None),
        P(("parts", "ep"), None, None),
        P(("parts", "ep"), None, None),
        P(("parts", "ep"), None),
        P(("parts", "ep"), None),
        P("parts"),
    )
    out_specs = (P(("parts", "ep"), None), P(("parts", "ep"), None))
    return jax.shard_map(shards, mesh=mesh, in_specs=in_specs, out_specs=out_specs, check_vma=False)
```

profile of v0, /device:TPU:9, one launch (start us, length us, event | category | flops | bytes accessed | tf_op | source)
XLA Modules:
  0.0 312.8 jit_solution(7199482188254444874)
XLA Ops:
  0.6 0.8 copy.33
  2.1 1.7 scatter_custom_fusion
  3.8 1.6 copy.35
  5.4 6.5 %all-to-all-start = ((bf16[16,16,2048]{2,0,1:T(8,128)(2,1)}), bf16[16,16,2048]{2,0,1:T(8,128)(2,1)}, u32[]{:S(2)}, u32[]{:S(2)}) async-start(bf16[16,16,2048]{2,0,1:T(8,128)(2,1)} %copy.35), calls=%async_computation | async-start | bytes 2097152 | tf_op jit(solution)/shard_map/all_to_all | solution.py:50
  12.0 8.9 %copy.36 = bf16[128,16,1536]{2,0,1:T(8,128)(2,1)} copy(bf16[128,16,1536]{2,1,0:T(8,128)(2,1)} %param.7) | data formatting | bytes 12582912 | tf_op args[1]
  20.9 16.1 %all-to-all-done = bf16[16,16,2048]{2,0,1:T(8,128)(2,1)} async-done(((bf16[16,16,2048]{2,0,1:T(8,128)(2,1)}), bf16[16,16,2048]{2,0,1:T(8,128)(2,1)}, u32[]{:S(2)}, u32[]{:S(2)}) %all-to-all-start) | async-done | bytes 1048608 | tf_op jit(solution)/shard_map/all_to_all | solution.py:50
  37.0 4.8 %all-to-all-start.1 = ((bf16[128,16,1536]{2,0,1:T(8,128)(2,1)}), bf16[128,16,1536]{2,0,1:T(8,128)(2,1)}, u32[]{:S(2)}, u32[]{:S(2)}) async-start(bf16[128,16,1536]{2,0,1:T(8,128)(2,1)} %copy.36), calls=%async_computation.1 | async-start | bytes 12582912 | tf_op jit(solution)/shard_map/all_to_all | solution.py:47
  41.8 3.4 %copy.37 = bf16[48,16,2048]{2,0,1:T(8,128)(2,1)} copy(bf16[48,16,2048]{2,1,0:T(8,128)(2,1)S(1)} %copy-done.1) | data formatting | bytes 6291456 | tf_op args[2]
  45.2 131.7 %all-to-all-done.1 = bf16[128,16,1536]{2,0,1:T(8,128)(2,1)} async-done(((bf16[128,16,1536]{2,0,1:T(8,128)(2,1)}), bf16[128,16,1536]{2,0,1:T(8,128)(2,1)}, u32[]{:S(2)}, u32[]{:S(2)}) %all-to-all-start.1) | async-done | bytes 6291488 | tf_op jit(solution)/shard_map/all_to_all | solution.py:47
  176.9 7.0 %all-to-all-start.2 = ((bf16[48,16,2048]{2,0,1:T(8,128)(2,1)}), bf16[48,16,2048]{2,0,1:T(8,128)(2,1)S(1)}, u32[]{:S(2)}, u32[]{:S(2)}) async-start(bf16[48,16,2048]{2,0,1:T(8,128)(2,1)} %copy.37), calls=%async_computation.2 | async-start | bytes 6291456 | tf_op jit(solution)/shard_map/all_to_all | solution.py:48
  184.0 0.6 scatter_custom_fusion.1
  187.2 6.1 %convolution_bitcast_fusion = f32[256,1,1536]{2,0,1:T(8,128)} fusion(bf16[256,2048]{1,0:T(8,128)(2,1)} %bitcast.6, bf16[2048,1536]{1,0:T(8,128)(2,1)} %bitcast.9), kind=kOutput, calls=%fused_computation.7 | convolution fusion | flops 1610612736 | bytes 8912896 | tf_op jit(solution)/shard_map/rjd,djf->rjf/dot_general | solution.py:10
  193.3 58.4 %all-to-all-done.2 = bf16[48,16,2048]{2,0,1:T(8,128)(2,1)S(1)} async-done(((bf16[48,16,2048]{2,0,1:T(8,128)(2,1)}), bf16[48,16,2048]{2,0,1:T(8,128)(2,1)S(1)}, u32[]{:S(2)}, u32[]{:S(2)}) %all-to-all-start.2) | async-done | bytes 3145760 | tf_op jit(solution)/shard_map/all_to_all | solution.py:48
  251.7 3.5 %fusion.2 = bf16[256,1,2048]{2,0,1:T(8,128)(2,1)} fusion(bf16[768,2048]{1,0:T(8,128)(2,1)S(1)} %bitcast.64, f32[256,1,1536]{2,0,1:T(8,128)} %convolution_bitcast_fusion), kind=kOutput, calls=%fused_computation.9 | convolution fusion | flops 807010304 | bytes 5767168 | tf_op jit(solution)/shard_map/rjf,fjd->rjd/dot_general | solution.py:15
  255.7 3.4 %reduce.4 = bf16[256,2048]{1,0:T(8,128)(2,1)} reduce(bf16[256,1,2048]{2,0,1:T(8,128)(2,1)} %fusion.2, bf16[]{:T(256)} %broadcast.120), dimensions={1}, to_apply=%copy.38.reduce_sub_computation | reduce | bytes 2097154 | tf_op jit(solution)/shard_map/convert_element_type | solution.py:17
  259.0 2.6 reshape.188
  261.7 6.9 %all-to-all-start.3 = ((bf16[16,2,16384]{2,1,0:T(2,128)(2,1)}), bf16[16,2,16384]{2,1,0:T(2,128)(2,1)}, u32[]{:S(2)}, u32[]{:S(2)}) async-start(bf16[16,2,16384]{2,1,0:T(2,128)(2,1)} %reshape.188), calls=%async_computation.3 | async-start | bytes 2097152 | tf_op jit(solution)/shard_map/all_to_all | solution.py:52
  269.0 3.4 %fusion = bf16[1536]{0:T(1024)(128)(2,1)S(1)} fusion(bf16[128,16,1536]{2,0,1:T(8,128)(2,1)} %all-to-all-done.1), kind=kLoop, calls=%fused_computation.4 | loop fusion | flops 6289920 | bytes 6294528 | tf_op jit(solution)/shard_map/reduce_max | solution.py:21
  272.4 32.2 %all-gather = f32[16,1,3584]{2,1,0:T(1,128)S(1)} all-gather(f32[1,1,3584]{2,1,0:T(1,128)S(1)} %maximum_bitcast_fusion), channel_id=1, replica_groups=mesh['parts'=2,'ep'=16] {'ep'}, dimensions={0}, use_global_device_ids=true | all-gather | bytes 243712 | tf_op jit(solution)/shard_map/all_gather | solution.py:58
  304.6 0.6 fusion.12
  305.2 4.3 %reshape.189 = bf16[256,1,2048]{2,1,0:T(2,128)(2,1)S(1)} reshape(bf16[16,2,16384]{2,1,0:T(2,128)(2,1)} %all-to-all-done.3) | data formatting | bytes 2097152
  309.5 0.6 copy.41
  310.7 0.9 gather_fusion
  311.7 1.1 fusion.3
  (27 shorter events, 2.8 us)
Async XLA Ops:
  0.6 1.4 copy-start
  5.4 31.6 %all-to-all-start = ((bf16[16,16,2048]{2,0,1:T(8,128)(2,1)}), bf16[16,16,2048]{2,0,1:T(8,128)(2,1)}, u32[]{:S(2)}, u32[]{:S(2)}) async-start(bf16[16,16,2048]{2,0,1:T(8,128)(2,1)} %copy.35), calls=%async_computation | async-start | bytes 2097152 | tf_op jit(solution)/shard_map/all_to_all | solution.py:50
  20.9 20.9 %copy-start.1 = (bf16[48,16,2048]{2,1,0:T(8,128)(2,1)S(1)}, bf16[48,16,2048]{2,1,0:T(8,128)(2,1)}, u32[]{:S(2)}) copy-start(bf16[48,16,2048]{2,1,0:T(8,128)(2,1)} %param.8) | copy-start | bytes 9437188
  37.0 139.9 %all-to-all-start.1 = ((bf16[128,16,1536]{2,0,1:T(8,128)(2,1)}), bf16[128,16,1536]{2,0,1:T(8,128)(2,1)}, u32[]{:S(2)}, u32[]{:S(2)}) async-start(bf16[128,16,1536]{2,0,1:T(8,128)(2,1)} %copy.36), calls=%async_computation.1 | async-start | bytes 12582912 | tf_op jit(solution)/shard_map/all_to_all | solution.py:47
  45.2 138.8 %copy-start.3 = (s32[16]{0:T(128)S(1)}, s32[16]{0:T(128)}, u32[]{:S(2)}) copy-start(s32[16]{0:T(128)} %param.11) | copy-start | bytes 196
  45.2 142.0 %copy-start.2 = (f32[16,8]{0,1:T(8,128)S(1)}, f32[16,8]{0,1:T(8,128)}, u32[]{:S(2)}) copy-start(f32[16,8]{0,1:T(8,128)} %param.10) | copy-start | bytes 1540
  176.9 74.8 %all-to-all-start.2 = ((bf16[48,16,2048]{2,0,1:T(8,128)(2,1)}), bf16[48,16,2048]{2,0,1:T(8,128)(2,1)S(1)}, u32[]{:S(2)}, u32[]{:S(2)}) async-start(bf16[48,16,2048]{2,0,1:T(8,128)(2,1)} %copy.37), calls=%async_computation.2 | async-start | bytes 6291456 | tf_op jit(solution)/shard_map/all_to_all | solution.py:48
  261.7 43.5 %all-to-all-start.3 = ((bf16[16,2,16384]{2,1,0:T(2,128)(2,1)}), bf16[16,2,16384]{2,1,0:T(2,128)(2,1)}, u32[]{:S(2)}, u32[]{:S(2)}) async-start(bf16[16,2,16384]{2,1,0:T(2,128)(2,1)} %reshape.188), calls=%async_computation.3 | async-start | bytes 2097152 | tf_op jit(solution)/shard_map/all_to_all | solution.py:52
where the time goes:
time: 314 us; the launch traced here: 313 us
  waiting for transfers between devices  206 us (66%)
  blocking collectives  32.2 us (10%)
  local copies, waits for them, and re-layouts  27.5 us (9%)
  starting transfers between devices  25.3 us (8%)
  matrix products  9.51 us (3%)
  other arithmetic  9.31 us (3%)
    all_to_all x1, waiting for transfers between devices, shards(): lax.all_to_all(gate_up, 'ep', split_axis=1, concat_axis=0, tiled=True)  132 us
    all_to_all x1, waiting for transfers between devices, shards(): lax.all_to_all(down_proj, 'ep', split_axis=1, concat_axis=0, tiled=True)  58.4 us
    all_gather x1, blocking collectives, shards(): every_row = lax.all_gather(scales, 'ep', axis=0, tiled=True)  32.2 us
    unnamed x15, local copies, waits for them, and re-layouts  20.7 us
    all_to_all x1, waiting for transfers between devices, shards(): lax.all_to_all(outbox, 'ep', split_axis=1, concat_axis=0, tiled=True)  16.1 us
    all_to_all x1, starting transfers between devices, shards(): lax.all_to_all(down_proj, 'ep', split_axis=1, concat_axis=0, tiled=True)  7.03 us
    all_to_all x1, starting transfers between devices, shards(): lax.all_to_all(expert_out, 'ep', split_axis=0, concat_axis=1, tiled=True)  6.93 us
    all_to_all x1, starting transfers between devices, shards(): lax.all_to_all(outbox, 'ep', split_axis=1, concat_axis=0, tiled=True)  6.55 us
  transfers between devices with their start and end apart: 4, of which 3 were waited for; matrix products, arithmetic and copies ran while one was open for 8% of the time, Pallas kernels for 0%

commit v1 on v0

--- a/solution.py
+++ b/solution.py
@@ -1,9 +1,18 @@
+import functools
 import math
 
 import jax
 import jax.numpy as jnp
 from jax import lax
+from jax.experimental import pallas as pl
+from jax.experimental.pallas import tpu as pltpu
 from jax.sharding import PartitionSpec as P
+
+
+LANES = 128
+CHUNKS = (2, 2, 2, 2)
+BLOCKS = 4
+OUT_STEPS = 4
 
 
 def expert_block(arrived, held_up, held_down):
@@ -25,7 +34,7 @@
     return jnp.concatenate([gate_scale, down_scale], axis=1)
 
 
-def shards(tokens, gate_up, down_proj, expert_ids, gate_weights, owner_slot):
+def owner_shards(tokens, gate_up, down_proj, expert_ids, gate_weights, owner_slot):
     tok_rows, model_width = tokens.shape
     top_count = expert_ids.shape[1]
     slots_all = gate_up.shape[1]
@@ -61,6 +70,450 @@
     return (moe_out, scales)
 
 
+def params(**kw):
+    return pltpu.CompilerParams(vmem_limit_bytes=58 * 1024 * 1024, **kw)
+
+
+def vmem():
+    return pl.BlockSpec(memory_space=pltpu.VMEM)
+
+
+def smem():
+    return pl.BlockSpec(memory_space=pltpu.SMEM)
+
+
+def pack_kernel(tok_ref, ids_ref, w_ref, out_ref):
+    n = out_ref.shape[0]
+    width = out_ref.shape[2] - LANES
+    top, rows = ids_ref.shape
+    w = w_ref[...]
+    w_hi = w.astype(jnp.bfloat16).astype(jnp.float32)
+    meta = jnp.concatenate(
+        [
+            ids_ref[...].astype(jnp.float32),
+            w_hi,
+            w - w_hi,
+            jnp.zeros((LANES - 3 * top, rows), jnp.float32),
+        ],
+        axis=0,
+    ).T.astype(jnp.bfloat16)
+    for d in range(n):
+        pair = d // 2
+        out_ref[d, :, :width] = tok_ref[:, pair * width : (pair + 1) * width]
+        out_ref[d, :, width:] = meta
+
+
+def prep_kernel(me_ref, gate_ref, send_ref, keep_ref):
+    rows, experts, cols = gate_ref.shape
+    turned = gate_ref[...].reshape(rows * experts, cols).T
+    half = keep_ref.shape[2]
+    parity = me_ref[0] % 2
+    for d in range(cols // half):
+        part = turned[d * half : (d + 1) * half]
+
+        @pl.when(parity == d % 2)
+        def _():
+            keep_ref[d // 2, 0] = part
+
+        @pl.when(parity != d % 2)
+        def _():
+            send_ref[d // 2, 0] = part
+
+
+def max_kernel(w_ref, max_ref):
+    top = jnp.abs(w_ref[0])
+    for r in range(1, w_ref.shape[0]):
+        top = jnp.maximum(top, jnp.abs(w_ref[r]))
+    max_ref[...] = top
+
+
+def lane_tables(got_ref, width, top):
+    turned = got_ref[...].astype(jnp.float32).T
+    ids = turned[width : width + top]
+    w = turned[width + top : width + 2 * top] + turned[width + 2 * top : width + 3 * top]
+    return turned[:width], ids, w
+
+
+def spread(values, experts):
+    rows, lanes = values.shape
+    pick = lax.broadcasted_iota(jnp.int32, (rows * experts, rows), 0) // experts
+    hot = (pick == lax.broadcasted_iota(jnp.int32, (rows * experts, rows), 1)).astype(
+        jnp.float32
+    ).astype(jnp.bfloat16)
+    wide = jnp.dot(hot, values.astype(jnp.bfloat16), preferred_element_type=jnp.float32)
+    return wide.astype(jnp.bfloat16).reshape(rows, experts, lanes)
+
+
+def named(ids, k, experts):
+    rows = lax.broadcasted_iota(jnp.int32, (experts, ids.shape[1]), 0).astype(jnp.float32)
+    return (rows == ids[k : k + 1]).astype(jnp.float32).astype(jnp.bfloat16)
+
+
+def hidden_kernel(first_k, per_k, top, experts, me_ref, got_ref, own_ref, pair_ref, *refs):
+    send_ref, keep_ref, own_x, pair_x = refs[-4:]
+    tokens = got_ref.shape[0]
+    blocks, rows, depth = own_ref.shape
+    width = depth // experts
+    step = pl.program_id(0)
+    me = me_ref[0]
+
+    @pl.when(step == 0)
+    def _():
+        columns, ids, _ = lane_tables(got_ref, 2 * width, top)
+        low, high = columns[:width], columns[width:]
+        first = me % 2 == 0
+        for x_ref, part in (
+            (own_x, jnp.where(first, low, high)),
+            (pair_x, jnp.where(first, high, low)),
+        ):
+            wide = spread(part, experts)
+            for k in range(per_k):
+                x_ref[:, :, k * tokens : (k + 1) * tokens] = wide * named(
+                    ids, first_k + k, experts
+                )
+
+    lanes = own_x.shape[2]
+    result = jnp.zeros((blocks * rows, lanes), jnp.float32)
+    for w_ref, x_ref in ((own_ref, own_x), (pair_ref, pair_x)):
+        result = result + jnp.dot(
+            w_ref[...].reshape(blocks * rows, depth),
+            x_ref[...].reshape(depth, lanes),
+            preferred_element_type=jnp.float32,
+        )
+    for b in range(blocks):
+        part = result[b * rows : (b + 1) * rows]
+        slot = (step * blocks + b) ^ (me // 2)
+
+        @pl.when(slot % 2 == 0)
+        def _():
+            keep_ref[slot // 2] = part
+
+        @pl.when(slot % 2 != 0)
+        def _():
+            send_ref[slot // 2] = part.astype(jnp.bfloat16)
+
+
+def left_terms(chunks, first_k, parts, top, experts, width, got_ref, pieces, left):
+    tokens = got_ref.shape[0]
+    half = pieces[0].shape[-2] // 2
+    _, ids, w = lane_tables(got_ref, width, top)
+    at = first_k
+    for c, per_k in enumerate(chunks):
+        hidden = pieces[c * parts][0].astype(jnp.float32)
+        for piece in pieces[c * parts + 1 : (c + 1) * parts]:
+            hidden = hidden + piece[0].astype(jnp.float32)
+        gate, up = hidden[:half], hidden[half:]
+        activated = gate / (1.0 + jnp.exp(-gate)) * up
+        for k in range(per_k):
+            mine = activated[:, k * tokens : (k + 1) * tokens] * w[at : at + 1]
+            term = spread(mine, experts) * named(ids, at, experts)
+            left = term if left is None else left + term
+            at += 1
+    return left
+
+
+def left_kernel(chunks, parts, top, experts, got_ref, *refs):
+    width = got_ref.shape[1] - LANES
+    refs[-1][...] = left_terms(chunks, 0, parts, top, experts, width, got_ref, refs[:-1], None)
+
+
+def down_kernel(chunk, first_k, parts, top, experts, base, *refs):
+    me_ref, slot_ref, got_ref, before_ref, down_ref, scale_ref = refs[:6]
+    pieces = refs[6:-3]
+    send_ref, keep_ref, left_ref = refs[-3:]
+    tokens = got_ref.shape[0]
+    width = got_ref.shape[1] - LANES
+
+    @pl.when(pl.program_id(0) == 0)
+    def _():
+        left = left_terms(
+            (chunk,), first_k, parts, top, experts, width, got_ref, pieces, before_ref[...]
+        )
+        left_ref[...] = left.reshape(-1, tokens).T
+
+    result = jnp.dot(left_ref[...], down_ref[...], preferred_element_type=jnp.float32)
+    me = me_ref[0]
+    count = send_ref.shape[0]
+    rows = tokens // (2 * count)
+    for d in range(2 * count):
+        slot = (d // 2) ^ (me // 2)
+
+        def put(out_ref):
+            for b in range(base // rows):
+                out_ref[slot, b * rows : (b + 1) * rows, :] = result[
+                    d * rows : (d + 1) * rows, b * LANES : (b + 1) * LANES
+                ]
+
+        pl.when(me % 2 == d % 2)(functools.partial(put, keep_ref))
+        pl.when(me % 2 != d % 2)(functools.partial(put, send_ref))
+
+    for e in range(experts):
+        slot = slot_ref[e] ^ me
+
+        @pl.when(slot % 2 == 0)
+        def _():
+            keep_ref[slot // 2, base:, :] = scale_ref[e, 0].astype(jnp.float32)
+
+        @pl.when(slot % 2 == 1)
+        def _():
+            send_ref[slot // 2, base:, :] = scale_ref[e, 0].astype(jnp.float32)
+
+
+def finish_kernel(gate_cols, gate_factor, down_factor, base, extra, *refs):
+    pieces, (out_ref, scale_ref) = refs[:-2], refs[-2:]
+    rows, _ = out_ref.shape
+    steps = pieces[0].shape[1] // (base + extra)
+    for s in range(steps):
+        low = s * (base + extra)
+        middle, high = low + base, low + base + extra
+        total = pieces[0][0, low:middle].astype(jnp.float32)
+        largest = pieces[0][0, middle:high].astype(jnp.float32)
+        for piece in pieces[1:]:
+            total = total + piece[0, low:middle].astype(jnp.float32)
+            largest = jnp.maximum(largest, piece[0, middle:high].astype(jnp.float32))
+        for q in range(base // rows):
+            at = (s * (base // rows) + q) * LANES
+            out_ref[:, at : at + LANES] = total[q * rows : (q + 1) * rows].astype(jnp.bfloat16)
+        for q in range(extra):
+            at = (s * extra + q) * LANES
+            if at < scale_ref.shape[1]:
+                factor = gate_factor if at < gate_cols else down_factor
+                scale_ref[:, at : at + LANES] = largest[q : q + 1] * factor
+
+
+def scatter(send, keep, n, first_bit, stages, merge):
+    whole, pieces, shift = [keep], [keep], first_bit
+    for stage, bits in enumerate(stages):
+        count = 2**bits
+        if stage:
+            split = [p.reshape((p.shape[0] // count, count) + p.shape[1:]) for p in pieces]
+            send = [merge([s[:, m] for s in split]) for m in range(1, count)]
+            pieces = [s[:, 0] for s in split]
+        for m in range(1, count):
+            got = lax.ppermute(
+                send[m - 1], "ep", [(i, i ^ (m << shift)) for i in range(n)]
+            )
+            whole.append(got)
+            pieces.append(got)
+        shift += bits
+    return whole
+
+
+def first_slot(piece):
+    return pl.BlockSpec((1,) + piece.shape[1:], lambda *_: (0,) * piece.ndim)
+
+
+def add_up(terms):
+    return sum(t.astype(jnp.float32) for t in terms).astype(jnp.bfloat16)
+
+
+def column_max(w, parts):
+    rows, experts, cols = w.shape
+    tile = cols // parts
+    return pl.pallas_call(
+        max_kernel,
+        grid=(parts,),
+        out_shape=jax.ShapeDtypeStruct((experts, cols), jnp.bfloat16),
+        in_specs=[pl.BlockSpec((rows, experts, tile), lambda i: (0, 0, i))],
+        out_specs=pl.BlockSpec((experts, tile), lambda i: (0, i)),
+        compiler_params=params(),
+        cost_estimate=pl.CostEstimate(
+            flops=2 * w.size, bytes_accessed=2 * w.size, transcendentals=0
+        ),
+    )(w)
+
+
+def row_shards(tokens, gate_up, down_proj, expert_ids, gate_weights, owner_slot):
+    return row_path(tokens, gate_up, down_proj, expert_ids, gate_weights, owner_slot)
+
+
+def row_path(tokens, gate_up, down_proj, expert_ids, gate_weights, owner_slot):
+    n = lax.axis_size("ep")
+    bits = n.bit_length() - 1
+    tok_rows, model_width = tokens.shape
+    top = expert_ids.shape[1]
+    gate_rows, experts, gate_cols = gate_up.shape
+    down_rows, _, _ = down_proj.shape
+    all_tokens = n * tok_rows
+    depth = gate_rows * experts
+    chunks = CHUNKS if top == sum(CHUNKS) else (top,)
+    me = lax.axis_index("ep").astype(jnp.int32).reshape(1)
+
+    packed = pl.pallas_call(
+        pack_kernel,
+        out_shape=jax.ShapeDtypeStruct((n, tok_rows, 2 * gate_rows + LANES), jnp.bfloat16),
+        in_specs=[vmem()] * 3,
+        out_specs=vmem(),
+        compiler_params=params(),
+    )(tokens, expert_ids.T, gate_weights.T)
+    got = lax.all_to_all(packed, "ep", split_axis=0, concat_axis=0, tiled=True)
+    got = got.reshape(all_tokens, 2 * gate_rows + LANES)
+
+    group = 8 if n % 8 == 0 else 4
+    per_half = n // group
+    half_block = pl.BlockSpec(
+        (group // 2, 1, down_rows, depth), lambda i: (i % per_half, i // per_half, 0, 0)
+    )
+    half_shape = jax.ShapeDtypeStruct((n // 2, 2, down_rows, depth), jnp.bfloat16)
+    send, own = pl.pallas_call(
+        prep_kernel,
+        grid=(2 * per_half,),
+        out_shape=(half_shape,) * 2,
+        in_specs=[
+            smem(),
+            pl.BlockSpec((gate_rows, experts, group * down_rows), lambda i: (0, 0, i)),
+        ],
+        out_specs=(half_block,) * 2,
+        compiler_params=params(),
+        cost_estimate=pl.CostEstimate(
+            flops=2 * gate_up.size, bytes_accessed=4 * gate_up.size, transcendentals=0
+        ),
+    )(me, gate_up)
+    pair = lax.ppermute(send, "ep", [(i, i ^ 1) for i in range(n)])
+    own = own.reshape(n // 2, 2 * down_rows, depth)
+    pair = pair.reshape(n // 2, 2 * down_rows, depth)
+
+    blocks = BLOCKS if (n // 2) % BLOCKS == 0 else 2
+    all_pieces, first_k = [], 0
+    for per_k in chunks:
+        lanes = per_k * all_tokens
+        shape = (n // 4, 2 * down_rows, lanes)
+        send, keep = pl.pallas_call(
+            functools.partial(hidden_kernel, first_k, per_k, top, experts),
+            grid=(n // 2 // blocks,),
+            out_shape=(
+                jax.ShapeDtypeStruct(shape, jnp.bfloat16),
+                jax.ShapeDtypeStruct(shape, jnp.float32),
+            ),
+            in_specs=[smem(), vmem()]
+            + [pl.BlockSpec((blocks, 2 * down_rows, depth), lambda i: (i, 0, 0))] * 2,
+            out_specs=(pl.BlockSpec(shape, lambda i: (0, 0, 0)),) * 2,
+            scratch_shapes=[pltpu.VMEM((gate_rows, experts, lanes), jnp.bfloat16)] * 2,
+            compiler_params=params(),
+            cost_estimate=pl.CostEstimate(
+                flops=2 * depth * gate_cols * lanes,
+                bytes_accessed=2 * depth * gate_cols + 3 * gate_cols * lanes // 2,
+                transcendentals=0,
+            ),
+        )(me, got, own, pair)
+        first_k += per_k
+        all_pieces += scatter([send], keep, n, 1, HIDDEN_STAGES(bits - 1), add_up)
+
+    parts = len(all_pieces) // len(chunks)
+    scale_cols = gate_cols + model_width
+    steps = OUT_STEPS if model_width % (OUT_STEPS * LANES) == 0 else 1
+    base = tok_rows * model_width // LANES // steps
+    extra = -(-scale_cols // (8 * steps * LANES)) * 8
+    gate_max = column_max(gate_up, 2)
+    down_max = column_max(down_proj, 2)
+    local_max = jnp.concatenate(
+        [
+            gate_max,
+            down_max,
+            jnp.zeros((experts, steps * extra * LANES - scale_cols), jnp.bfloat16),
+        ],
+        axis=1,
+    ).reshape(experts, steps, extra, LANES)
+
+    early, late = all_pieces[:-parts], all_pieces[-parts:]
+    before = pl.pallas_call(
+        functools.partial(left_kernel, chunks[:-1], parts, top, experts),
+        grid=(1,),
+        out_shape=jax.ShapeDtypeStruct((down_rows, experts, all_tokens), jnp.bfloat16),
+        in_specs=[vmem()] + [first_slot(p) for p in early],
+        out_specs=vmem(),
+        compiler_params=params(),
+    )(got, *early)
+    shape = (n // 2, steps * (base + extra), LANES)
+    out_block = pl.BlockSpec((n // 2, base + extra, LANES), lambda i: (0, i, 0))
+    send, keep = pl.pallas_call(
+        functools.partial(
+            down_kernel, chunks[-1], top - chunks[-1], parts, top, experts, base
+        ),
+        grid=(steps,),
+        out_shape=(jax.ShapeDtypeStruct(shape, jnp.float32),) * 2,
+        in_specs=[
+            smem(),
+            smem(),
+            vmem(),
+            vmem(),
+            pl.BlockSpec((down_rows * experts, model_width // steps), lambda i: (0, i)),
+            pl.BlockSpec((experts, 1, extra, LANES), lambda i: (0, i, 0, 0)),
+        ]
+        + [first_slot(p) for p in late],
+        out_specs=(out_block,) * 2,
+        scratch_shapes=[pltpu.VMEM((all_tokens, down_rows * experts), jnp.bfloat16)],
+        compiler_params=params(),
+    )(
+        me,
+        owner_slot,
+        got,
+        before,
+        down_proj.reshape(down_rows * experts, model_width),
+        local_max,
+        *late,
+    )
+
+    def merge(terms):
+        row = lax.broadcasted_iota(jnp.int32, terms[0].shape, 1) % (base + extra)
+        terms = [t.astype(jnp.float32) for t in terms]
+        return jnp.where(row < base, sum(terms), functools.reduce(jnp.maximum, terms)).astype(
+            jnp.bfloat16
+        )
+
+    pieces = scatter([send], keep, n, 0, OUTPUT_STAGES(bits), merge)
+    return pl.pallas_call(
+        functools.partial(
+            finish_kernel,
+            gate_cols,
+            math.sqrt(gate_rows * n),
+            math.sqrt(down_rows * n),
+            base,
+            extra,
+        ),
+        grid=(1,),
+        out_shape=(
+            jax.ShapeDtypeStruct((tok_rows, model_width), jnp.bfloat16),
+            jax.ShapeDtypeStruct((1, scale_cols), jnp.float32),
+        ),
+        in_specs=[first_slot(p) for p in pieces],
+        out_specs=(vmem(),) * 2,
+        compiler_params=params(),
+    )(*pieces)
+
+
+def HIDDEN_STAGES(bits):
+    return [1] * bits
+
+
+def OUTPUT_STAGES(bits):
+    return [1] * bits
+
+
+def shards(tokens, gate_up, down_proj, expert_ids, gate_weights, owner_slot):
+    n = lax.axis_size("ep")
+    tok_rows, model_width = tokens.shape
+    top = expert_ids.shape[1]
+    gate_rows, experts, gate_cols = gate_up.shape
+    down_rows = down_proj.shape[0]
+    fits = (
+        n >= 2
+        and n & (n - 1) == 0
+        and experts == n
+        and experts % 16 == 0
+        and tok_rows % 16 == 0
+        and gate_rows % LANES == 0
+        and down_rows % 16 == 0
+        and n % 4 == 0
+        and model_width % LANES == 0
+        and gate_cols % LANES == 0
+        and 3 * top <= LANES
+        and experts <= 256
+    )
+    path = row_shards if fits else owner_shards
+    return path(tokens, gate_up, down_proj, expert_ids, gate_weights, owner_slot)
+
+
 def solution(mesh):
     in_specs = (
         P(("parts", "ep"), None),
@@ -71,4 +524,6 @@
         P("parts"),
     )
     out_specs = (P(("parts", "ep"), None), P(("parts", "ep"), None))
-    return jax.shard_map(shards, mesh=mesh, in_specs=in_specs, out_specs=out_specs, check_vma=False)
+    return jax.shard_map(
+        shards, mesh=mesh, in_specs=in_specs, out_specs=out_specs, check_vma=False
+    )

time: 314 us -> 151 us (0.48)
  the two profiles are of different devices: /device:TPU:9 before, /device:TPU:0 now
where the time goes in v1:
time: 151 us
  waiting for transfers between devices  63.4 us (42%)
  Pallas kernels  56.9 us (38%)
  starting transfers between devices  21.4 us (14%)
  local copies, waits for them, and re-layouts  5.69 us (4%)
  other arithmetic  2.41 us (2%)
    ppermute x16, waiting for transfers between devices, scatter(): lax.ppermute(send[m - 1], 'ep', [(i, i ^ m << shift) for i in range(n)])  60.7 us
    pallas_call x4, Pallas kernels, row_path(): pl.pallas_call(functools.partial(hidden_kernel, first_k, per_k, top, expe...  30.2 us
    ppermute x16, starting transfers between devices, scatter(): lax.ppermute(send[m - 1], 'ep', [(i, i ^ m << shift) for i in range(n)])  13.9 us
    pallas_call x1, Pallas kernels, row_path(): pl.pallas_call(prep_kernel, grid=(2 * per_half,), out_shape=(half_shape,)...  7.04 us
    all_to_all x1, starting transfers between devices, row_path(): got = lax.all_to_all(packed, 'ep', split_axis=0, concat_axis=0, tiled=True)  7 us
    pallas_call x1, Pallas kernels, row_path(): pl.pallas_call(functools.partial(down_kernel, chunks[-1], top - chunks[-1...  6.84 us
    pallas_call x2, Pallas kernels, column_max(): pl.pallas_call(max_kernel, grid=(parts,), out_shape=jax.ShapeDtypeStruct(...  6.27 us
    unnamed x53, local copies, waits for them, and re-layouts  3.32 us
  transfers between devices with their start and end apart: 18, of which 13 were waited for; matrix products, arithmetic and copies ran while one was open for 2% of the time, Pallas kernels for 7%

profile of v1, /device:TPU:0, one launch (start us, length us, event | category | flops | bytes accessed | tf_op | source)
XLA Modules:
  0.0 150.8 jit_solution(8911284902207612802)
XLA Ops:
  0.6 7.0 %shard_map.78 = (bf16[8,2,48,2048]{3,2,1,0:T(8,128)(2,1)}, bf16[8,2,48,2048]{3,2,1,0:T(8,128)(2,1)}) custom-call(s32[1]{0:T(128)} %bitcast.me_ref.refs_0_, bf16[128,16,1536]{2,1,0:T(8,128)(2,1)} %w_ref.2), custom_call_target="tpu_custom_call" | custom-call | flops 6291456 | bytes 12582912 | tf_op jit(solution)/shard_map/pallas_call | solution.py:358
  9.8 7.0 %all-to-all-start = ((bf16[16,16,384]{2,1,0:T(8,128)(2,1)}), bf16[16,16,384]{2,1,0:T(8,128)(2,1)S(1)}, u32[]{:S(2)}, u32[]{:S(2)}) async-start(bf16[16,16,384]{2,1,0:T(8,128)(2,1)} %shard_map.77), calls=%async_computation | async-start | bytes 393216 | tf_op jit(solution)/shard_map/all_to_all | solution.py:349
  16.8 2.6 %shard_map.84 = bf16[16,2048]{1,0:T(8,128)(2,1)} custom-call(bf16[48,16,2048]{2,1,0:T(8,128)(2,1)} %w_ref.3), custom_call_target="tpu_custom_call" | custom-call | flops 3145728 | bytes 3145728 | tf_op jit(solution)/shard_map/pallas_call | solution.py:313
  19.4 3.7 %shard_map.83 = bf16[16,1536]{1,0:T(8,128)(2,1)} custom-call(bf16[128,16,1536]{2,1,0:T(8,128)(2,1)} %w_ref.2), custom_call_target="tpu_custom_call" | custom-call | flops 6291456 | bytes 6291456 | tf_op jit(solution)/shard_map/pallas_call | solution.py:313
  23.1 2.7 %all-to-all-done = bf16[16,16,384]{2,1,0:T(8,128)(2,1)S(1)} async-done(((bf16[16,16,384]{2,1,0:T(8,128)(2,1)}), bf16[16,16,384]{2,1,0:T(8,128)(2,1)S(1)}, u32[]{:S(2)}, u32[]{:S(2)}) %all-to-all-start) | async-done | bytes 196640 | tf_op jit(solution)/shard_map/all_to_all | solution.py:349
  26.4 7.5 %shard_map.81 = (bf16[4,96,512]{2,1,0:T(8,128)(2,1)}, f32[4,96,512]{2,1,0:T(8,128)}) custom-call(s32[1]{0:T(128)} %bitcast.me_ref.refs_0_, bf16[256,384]{1,0:T(8,128)(2,1)} %bitcast.200, bf16[8,96,2048]{2,1,0:T(8,128)(2,1)} %bitcast.224, bf16[8,96,2048]{2,1,0:T(8,128)(2,1)} %bitcast.5.pair_ref), custom_call_target="tpu_custom_call" | custom-call | flops 3221225472 | bytes 7471104 | tf_op jit(solution)/shard_map/pallas_call | solution.py:381
  34.0 7.6 %shard_map.80 = (bf16[4,96,512]{2,1,0:T(8,128)(2,1)}, f32[4,96,512]{2,1,0:T(8,128)}) custom-call(s32[1]{0:T(128)} %bitcast.me_ref.refs_0_, bf16[256,384]{1,0:T(8,128)(2,1)} %bitcast.201, bf16[8,96,2048]{2,1,0:T(8,128)(2,1)} %bitcast.225, bf16[8,96,2048]{2,1,0:T(8,128)(2,1)} %bitcast.5.pair_ref), custom_call_target="tpu_custom_call" | custom-call | flops 3221225472 | bytes 7471104 | tf_op jit(solution)/shard_map/pallas_call | solution.py:381
  41.5 7.5 %shard_map.79 = (bf16[4,96,512]{2,1,0:T(8,128)(2,1)}, f32[4,96,512]{2,1,0:T(8,128)}) custom-call(s32[1]{0:T(128)} %bitcast.me_ref.refs_0_, bf16[256,384]{1,0:T(8,128)(2,1)} %bitcast.202, bf16[8,96,2048]{2,1,0:T(8,128)(2,1)} %bitcast.226, bf16[8,96,2048]{2,1,0:T(8,128)(2,1)} %bitcast.5.pair_ref), custom_call_target="tpu_custom_call" | custom-call | flops 3221225472 | bytes 7471104 | tf_op jit(solution)/shard_map/pallas_call | solution.py:381
  49.0 7.6 %shard_map.85 = (bf16[4,96,512]{2,1,0:T(8,128)(2,1)}, f32[4,96,512]{2,1,0:T(8,128)}) custom-call(s32[1]{0:T(128)} %bitcast.me_ref.refs_0_, bf16[256,384]{1,0:T(8,128)(2,1)} %bitcast.203, bf16[8,96,2048]{2,1,0:T(8,128)(2,1)} %bitcast.227, bf16[8,96,2048]{2,1,0:T(8,128)(2,1)} %bitcast.5.pair_ref), custom_call_target="tpu_custom_call" | custom-call | flops 3221225472 | bytes 7471104 | tf_op jit(solution)/shard_map/pallas_call | solution.py:381
  56.8 2.1 %collective-permute-start.4 = (bf16[4,96,512]{2,1,0:T(8,128)(2,1)S(1)}, bf16[4,96,512]{2,1,0:T(8,128)(2,1)S(1)}, u32[]{:S(2)}, u32[]{:S(2)}) collective-permute-start(bf16[4,96,512]{2,1,0:T(8,128)(2,1)S(1)} %copy-done.24), channel_id=1, source_target_pairs={{0,2},{1,3},{2,0},{3,1},{4,6},{5,7},{6,4},{7,5},{8,10},{9,11},{10,... | collective-permute-start | bytes 1179656 | tf_op jit(solution)/shard_map/ppermute | solution.py:293
  62.0 6.6 %collective-permute-done.7.refs_9_ = bf16[4,96,512]{2,1,0:T(8,128)(2,1)S(1)} collective-permute-done((bf16[4,96,512]{2,1,0:T(8,128)(2,1)S(1)}, bf16[4,96,512]{2,1,0:T(8,128)(2,1)S(1)}, u32[]{:S(2)}, u32[]{:S(2)}) %collective-permute-start.7) | collective-permute-done | bytes 393248 | tf_op jit(solution)/shard_map/ppermute | solution.py:293
  68.8 8.3 %collective-permute-done.4.refs_5_ = bf16[4,96,512]{2,1,0:T(8,128)(2,1)S(1)} collective-permute-done((bf16[4,96,512]{2,1,0:T(8,128)(2,1)S(1)}, bf16[4,96,512]{2,1,0:T(8,128)(2,1)S(1)}, u32[]{:S(2)}, u32[]{:S(2)}) %collective-permute-start.4) | collective-permute-done | bytes 393248 | tf_op jit(solution)/shard_map/ppermute | solution.py:293
  77.3 8.3 %collective-permute-done.1.refs_1_ = bf16[4,96,512]{2,1,0:T(8,128)(2,1)S(1)} collective-permute-done((bf16[4,96,512]{2,1,0:T(8,128)(2,1)S(1)}, bf16[4,96,512]{2,1,0:T(8,128)(2,1)S(1)}, u32[]{:S(2)}, u32[]{:S(2)}) %collective-permute-start.1) | collective-permute-done | bytes 393248 | tf_op jit(solution)/shard_map/ppermute | solution.py:293
  85.7 7.0 %collective-permute-done.10.refs_7_ = bf16[4,96,512]{2,1,0:T(8,128)(2,1)S(1)} collective-permute-done((bf16[4,96,512]{2,1,0:T(8,128)(2,1)}, bf16[4,96,512]{2,1,0:T(8,128)(2,1)S(1)}, u32[]{:S(2)}, u32[]{:S(2)}) %collective-permute-start.10) | collective-permute-done | bytes 393248 | tf_op jit(solution)/shard_map/ppermute | solution.py:293
  98.1 2.3 %collective-permute-done.11.refs_8_ = bf16[2,96,512]{2,1,0:T(8,128)(2,1)S(1)} collective-permute-done((bf16[2,96,512]{2,1,0:T(8,128)(2,1)S(1)}, bf16[2,96,512]{2,1,0:T(8,128)(2,1)S(1)}, u32[]{:S(2)}, u32[]{:S(2)}) %collective-permute-start.11) | collective-permute-done | bytes 196640 | tf_op jit(solution)/shard_map/ppermute | solution.py:293
  103.0 4.8 %collective-permute-done.9.refs_11_ = bf16[1,96,512]{2,1,0:T(8,128)(2,1)S(1)} collective-permute-done((bf16[1,96,512]{2,1,0:T(8,128)(2,1)S(1)}, bf16[1,96,512]{2,1,0:T(8,128)(2,1)S(1)}, u32[]{:S(2)}, u32[]{:S(2)}) %collective-permute-start.9) | collective-permute-done | bytes 98336 | tf_op jit(solution)/shard_map/ppermute | solution.py:293
  107.7 2.1 %collective-permute-done.6.refs_7_ = bf16[1,96,512]{2,1,0:T(8,128)(2,1)S(1)} collective-permute-done((bf16[1,96,512]{2,1,0:T(8,128)(2,1)S(1)}, bf16[1,96,512]{2,1,0:T(8,128)(2,1)S(1)}, u32[]{:S(2)}, u32[]{:S(2)}) %collective-permute-start.6) | collective-permute-done | bytes 98336 | tf_op jit(solution)/shard_map/ppermute | solution.py:293
  109.8 2.1 %collective-permute-done.3.refs_3_ = bf16[1,96,512]{2,1,0:T(8,128)(2,1)S(1)} collective-permute-done((bf16[1,96,512]{2,1,0:T(8,128)(2,1)S(1)}, bf16[1,96,512]{2,1,0:T(8,128)(2,1)S(1)}, u32[]{:S(2)}, u32[]{:S(2)}) %collective-permute-start.3) | collective-permute-done | bytes 98336 | tf_op jit(solution)/shard_map/ppermute | solution.py:293
  112.6 3.1 %shard_map.82.refs_3_ = bf16[48,16,256]{2,1,0:T(8,128)(2,1)} custom-call(bf16[256,384]{1,0:T(8,128)(2,1)} %bitcast.204, f32[4,96,512]{2,1,0:T(8,128)} %get-tuple-element.16.refs_0_, bf16[4,96,512]{2,1,0:T(8,128)(2,1)} %copy-done.9, bf16[2,96,512]{2,1,0:T(8,128)(2,1)} %copy-done.14, bf16[1,96,512]{2,1,0:T(8,128)(2,1)} %copy-done.21, ...), custom_call_target="tpu_custom_call" | custom-call | tf_op jit(solution)/shard_map/pallas_call | solution.py:419
  116.4 6.8 %shard_map.86 = (f32[8,288,128]{2,1,0:T(8,128)}, f32[8,288,128]{2,1,0:T(8,128)}) custom-call(s32[1]{0:T(128)} %bitcast.me_ref.refs_0_, s32[16]{0:T(128)} %refs_1_.1, bf16[256,384]{1,0:T(8,128)(2,1)} %bitcast.205, bf16[48,16,256]{2,1,0:T(8,128)(2,1)} %shard_map.82.refs_3_, bf16[768,2048]{1,0:T(8,128)(2,1)} %bitcast.183, bf16[16,4,8,128]{3,2,1,0:T(8,128)(2,1)} %bitcast.216, ...), custom_call_target="tpu_custom_call" | custom-call | tf_op jit(solution)/shard_map/pallas_call | solution.py:429
  123.3 3.0 %collective-permute-done.13.refs_1_ = f32[8,288,128]{2,1,0:T(8,128)S(1)} collective-permute-done((f32[8,288,128]{2,1,0:T(8,128)}, f32[8,288,128]{2,1,0:T(8,128)S(1)}, u32[]{:S(2)}, u32[]{:S(2)}) %collective-permute-start.13) | collective-permute-done | bytes 1179680 | tf_op jit(solution)/shard_map/ppermute | solution.py:293
  130.7 6.3 %collective-permute-done.14.refs_2_ = bf16[4,288,128]{2,1,0:T(8,128)(2,1)S(1)} collective-permute-done((bf16[4,288,128]{2,1,0:T(8,128)(2,1)S(1)}, bf16[4,288,128]{2,1,0:T(8,128)(2,1)S(1)}, u32[]{:S(2)}, u32[]{:S(2)}) %collective-permute-start.14) | collective-permute-done | bytes 294944 | tf_op jit(solution)/shard_map/ppermute | solution.py:293
  137.4 5.1 %collective-permute-done.15.refs_3_ = bf16[2,288,128]{2,1,0:T(8,128)(2,1)S(1)} collective-permute-done((bf16[2,288,128]{2,1,0:T(8,128)(2,1)S(1)}, bf16[2,288,128]{2,1,0:T(8,128)(2,1)S(1)}, u32[]{:S(2)}, u32[]{:S(2)}) %collective-permute-start.15) | collective-permute-done | bytes 147488 | tf_op jit(solution)/shard_map/ppermute | solution.py:293
  143.6 4.8 %collective-permute-done.16.refs_4_ = bf16[1,288,128]{2,1,0:T(8,128)(2,1)S(1)} collective-permute-done((bf16[1,288,128]{2,1,0:T(8,128)(2,1)S(1)}, bf16[1,288,128]{2,1,0:T(8,128)(2,1)S(1)}, u32[]{:S(2)}, u32[]{:S(2)}) %collective-permute-start.16) | collective-permute-done | bytes 73760 | tf_op jit(solution)/shard_map/ppermute | solution.py:293
  (104 shorter events, 23.8 us)
Async XLA Ops:
  7.7 18.1 %collective-permute-start = (bf16[8,2,48,2048]{3,2,1,0:T(8,128)(2,1)}, bf16[8,2,48,2048]{3,2,1,0:T(8,128)(2,1)}, u32[]{:S(2)}, u32[]{:S(2)}) collective-permute-start(bf16[8,2,48,2048]{3,2,1,0:T(8,128)(2,1)} %get-tuple-element.15), channel_id=1, source_target_pairs={{0,1},{1,0},{2,3},{3,2},{4,5},{5,4},{6,7},{7,6},{8,9},{9,8},{10,11... | collective-permute-start | bytes 9437192 | tf_op jit(solution)/shard_map/ppermute | solution.py:372
  9.8 16.0 %all-to-all-start = ((bf16[16,16,384]{2,1,0:T(8,128)(2,1)}), bf16[16,16,384]{2,1,0:T(8,128)(2,1)S(1)}, u32[]{:S(2)}, u32[]{:S(2)}) async-start(bf16[16,16,384]{2,1,0:T(8,128)(2,1)} %shard_map.77), calls=%async_computation | async-start | bytes 393216 | tf_op jit(solution)/shard_map/all_to_all | solution.py:349
  56.7 12.0 %collective-permute-start.7 = (bf16[4,96,512]{2,1,0:T(8,128)(2,1)S(1)}, bf16[4,96,512]{2,1,0:T(8,128)(2,1)S(1)}, u32[]{:S(2)}, u32[]{:S(2)}) collective-permute-start(bf16[4,96,512]{2,1,0:T(8,128)(2,1)S(1)} %copy-done.25), channel_id=1, source_target_pairs={{0,2},{1,3},{2,0},{3,1},{4,6},{5,7},{6,4},{7,5},{8,10},{9,11},{10,... | collective-permute-start | bytes 1179656 | tf_op jit(solution)/shard_map/ppermute | solution.py:293
  56.7 36.0 %copy-start.4 = (f32[4,96,512]{2,1,0:T(8,128)S(1)}, f32[4,96,512]{2,1,0:T(8,128)}, u32[]{:S(2)}) copy-start(f32[4,96,512]{2,1,0:T(8,128)} %get-tuple-element.22.refs_6_) | copy-start | bytes 2359300
  56.8 20.3 %collective-permute-start.4 = (bf16[4,96,512]{2,1,0:T(8,128)(2,1)S(1)}, bf16[4,96,512]{2,1,0:T(8,128)(2,1)S(1)}, u32[]{:S(2)}, u32[]{:S(2)}) collective-permute-start(bf16[4,96,512]{2,1,0:T(8,128)(2,1)S(1)} %copy-done.24), channel_id=1, source_target_pairs={{0,2},{1,3},{2,0},{3,1},{4,6},{5,7},{6,4},{7,5},{8,10},{9,11},{10,... | collective-permute-start | bytes 1179656 | tf_op jit(solution)/shard_map/ppermute | solution.py:293
  58.9 26.7 %collective-permute-start.1 = (bf16[4,96,512]{2,1,0:T(8,128)(2,1)S(1)}, bf16[4,96,512]{2,1,0:T(8,128)(2,1)S(1)}, u32[]{:S(2)}, u32[]{:S(2)}) collective-permute-start(bf16[4,96,512]{2,1,0:T(8,128)(2,1)S(1)} %copy-done.23), channel_id=1, source_target_pairs={{0,2},{1,3},{2,0},{3,1},{4,6},{5,7},{6,4},{7,5},{8,10},{9,11},{10,... | collective-permute-start | bytes 1179656 | tf_op jit(solution)/shard_map/ppermute | solution.py:293
  59.0 33.8 %collective-permute-start.10 = (bf16[4,96,512]{2,1,0:T(8,128)(2,1)}, bf16[4,96,512]{2,1,0:T(8,128)(2,1)S(1)}, u32[]{:S(2)}, u32[]{:S(2)}) collective-permute-start(bf16[4,96,512]{2,1,0:T(8,128)(2,1)} %get-tuple-element.23), channel_id=1, source_target_pairs={{0,2},{1,3},{2,0},{3,1},{4,6},{5,7},{6,4},{7,5},{8,10},{9,11},{10,... | collective-permute-start | bytes 1179656 | tf_op jit(solution)/shard_map/ppermute | solution.py:293
  68.7 31.8 %copy-start.7 = (bf16[4,96,512]{2,1,0:T(8,128)(2,1)}, bf16[4,96,512]{2,1,0:T(8,128)(2,1)S(1)}, u32[]{:S(2)}) copy-start(bf16[4,96,512]{2,1,0:T(8,128)(2,1)S(1)} %collective-permute-done.7.refs_9_) | copy-start | bytes 1179652
  68.7 33.5 %copy-start.16 = (bf16[16,2048]{1,0:T(8,128)(2,1)S(1)}, bf16[16,2048]{1,0:T(8,128)(2,1)}, u32[]{:S(2)}) copy-start(bf16[16,2048]{1,0:T(8,128)(2,1)} %shard_map.84) | copy-start | bytes 196612
  68.7 33.5 %copy-start.17 = (bf16[16,1536]{1,0:T(8,128)(2,1)S(1)}, bf16[16,1536]{1,0:T(8,128)(2,1)}, u32[]{:S(2)}) copy-start(bf16[16,1536]{1,0:T(8,128)(2,1)} %shard_map.83) | copy-start | bytes 147460
  68.7 24.4 %collective-permute-start.8 = (bf16[2,96,512]{2,1,0:T(8,128)(2,1)S(1)}, bf16[2,96,512]{2,1,0:T(8,128)(2,1)S(1)}, u32[]{:S(2)}, u32[]{:S(2)}) collective-permute-start(bf16[2,96,512]{2,1,0:T(8,128)(2,1)S(1)} %fusion.15), channel_id=1, source_target_pairs={{0,4},{1,5},{2,6},{3,7},{4,0},{5,1},{6,2},{7,3},{8,12},{9,13},{10,... | collective-permute-start | bytes 589832 | tf_op jit(solution)/shard_map/ppermute | solution.py:293
  77.1 25.9 %copy-start.8 = (bf16[4,96,512]{2,1,0:T(8,128)(2,1)}, bf16[4,96,512]{2,1,0:T(8,128)(2,1)S(1)}, u32[]{:S(2)}) copy-start(bf16[4,96,512]{2,1,0:T(8,128)(2,1)S(1)} %collective-permute-done.4.refs_5_) | copy-start | bytes 1179652
  77.2 17.8 %collective-permute-start.5 = (bf16[2,96,512]{2,1,0:T(8,128)(2,1)S(1)}, bf16[2,96,512]{2,1,0:T(8,128)(2,1)S(1)}, u32[]{:S(2)}, u32[]{:S(2)}) collective-permute-start(bf16[2,96,512]{2,1,0:T(8,128)(2,1)S(1)} %fusion.14), channel_id=1, source_target_pairs={{0,4},{1,5},{2,6},{3,7},{4,0},{5,1},{6,2},{7,3},{8,12},{9,13},{10,... | collective-permute-start | bytes 589832 | tf_op jit(solution)/shard_map/ppermute | solution.py:293
  85.5 26.4 %copy-start.9 = (bf16[4,96,512]{2,1,0:T(8,128)(2,1)}, bf16[4,96,512]{2,1,0:T(8,128)(2,1)S(1)}, u32[]{:S(2)}) copy-start(bf16[4,96,512]{2,1,0:T(8,128)(2,1)S(1)} %collective-permute-done.1.refs_1_) | copy-start | bytes 1179652
  85.6 10.8 %collective-permute-start.2 = (bf16[2,96,512]{2,1,0:T(8,128)(2,1)S(1)}, bf16[2,96,512]{2,1,0:T(8,128)(2,1)S(1)}, u32[]{:S(2)}, u32[]{:S(2)}) collective-permute-start(bf16[2,96,512]{2,1,0:T(8,128)(2,1)S(1)} %fusion.13), channel_id=1, source_target_pairs={{0,4},{1,5},{2,6},{3,7},{4,0},{5,1},{6,2},{7,3},{8,12},{9,13},{10,... | collective-permute-start | bytes 589832 | tf_op jit(solution)/shard_map/ppermute | solution.py:293
  92.8 7.7 %collective-permute-start.11 = (bf16[2,96,512]{2,1,0:T(8,128)(2,1)S(1)}, bf16[2,96,512]{2,1,0:T(8,128)(2,1)S(1)}, u32[]{:S(2)}, u32[]{:S(2)}) collective-permute-start(bf16[2,96,512]{2,1,0:T(8,128)(2,1)S(1)} %fusion.16), channel_id=1, source_target_pairs={{0,4},{1,5},{2,6},{3,7},{4,0},{5,1},{6,2},{7,3},{8,12},{9,13},{10,... | collective-permute-start | bytes 589832 | tf_op jit(solution)/shard_map/ppermute | solution.py:293
  93.2 14.5 %collective-permute-start.9 = (bf16[1,96,512]{2,1,0:T(8,128)(2,1)S(1)}, bf16[1,96,512]{2,1,0:T(8,128)(2,1)S(1)}, u32[]{:S(2)}, u32[]{:S(2)}) collective-permute-start(bf16[1,96,512]{2,1,0:T(8,128)(2,1)S(1)} %fusion.31), channel_id=1, source_target_pairs={{0,8},{1,9},{2,10},{3,11},{4,12},{5,13},{6,14},{7,15},{8,0},{9,1},... | collective-permute-start | bytes 294920 | tf_op jit(solution)/shard_map/ppermute | solution.py:293
  95.0 14.8 %collective-permute-start.6 = (bf16[1,96,512]{2,1,0:T(8,128)(2,1)S(1)}, bf16[1,96,512]{2,1,0:T(8,128)(2,1)S(1)}, u32[]{:S(2)}, u32[]{:S(2)}) collective-permute-start(bf16[1,96,512]{2,1,0:T(8,128)(2,1)S(1)} %fusion.30), channel_id=1, source_target_pairs={{0,8},{1,9},{2,10},{3,11},{4,12},{5,13},{6,14},{7,15},{8,0},{9,1},... | collective-permute-start | bytes 294920 | tf_op jit(solution)/shard_map/ppermute | solution.py:293
  96.4 15.5 %collective-permute-start.3 = (bf16[1,96,512]{2,1,0:T(8,128)(2,1)S(1)}, bf16[1,96,512]{2,1,0:T(8,128)(2,1)S(1)}, u32[]{:S(2)}, u32[]{:S(2)}) collective-permute-start(bf16[1,96,512]{2,1,0:T(8,128)(2,1)S(1)} %fusion.29), channel_id=1, source_target_pairs={{0,8},{1,9},{2,10},{3,11},{4,12},{5,13},{6,14},{7,15},{8,0},{9,1},... | collective-permute-start | bytes 294920 | tf_op jit(solution)/shard_map/ppermute | solution.py:293
  100.5 15.2 %collective-permute-start.12 = (bf16[1,96,512]{2,1,0:T(8,128)(2,1)S(1)}, bf16[1,96,512]{2,1,0:T(8,128)(2,1)S(1)}, u32[]{:S(2)}, u32[]{:S(2)}) collective-permute-start(bf16[1,96,512]{2,1,0:T(8,128)(2,1)S(1)} %fusion.32), channel_id=1, source_target_pairs={{0,8},{1,9},{2,10},{3,11},{4,12},{5,13},{6,14},{7,15},{8,0},{9,1},... | collective-permute-start | bytes 294920 | tf_op jit(solution)/shard_map/ppermute | solution.py:293
  123.2 3.1 %collective-permute-start.13 = (f32[8,288,128]{2,1,0:T(8,128)}, f32[8,288,128]{2,1,0:T(8,128)S(1)}, u32[]{:S(2)}, u32[]{:S(2)}) collective-permute-start(f32[8,288,128]{2,1,0:T(8,128)} %get-tuple-element.25), channel_id=1, source_target_pairs={{0,1},{1,0},{2,3},{3,2},{4,5},{5,4},{6,7},{7,6},{8,9},{9,8},{10,11... | collective-permute-start | bytes 3538952 | tf_op jit(solution)/shard_map/ppermute | solution.py:293
  127.9 9.1 %collective-permute-start.14 = (bf16[4,288,128]{2,1,0:T(8,128)(2,1)S(1)}, bf16[4,288,128]{2,1,0:T(8,128)(2,1)S(1)}, u32[]{:S(2)}, u32[]{:S(2)}) collective-permute-start(bf16[4,288,128]{2,1,0:T(8,128)(2,1)S(1)} %fusion), channel_id=1, source_target_pairs={{0,2},{1,3},{2,0},{3,1},{4,6},{5,7},{6,4},{7,5},{8,10},{9,11},{10,... | collective-permute-start | bytes 884744 | tf_op jit(solution)/shard_map/ppermute | solution.py:293
  137.3 5.2 %collective-permute-start.15 = (bf16[2,288,128]{2,1,0:T(8,128)(2,1)S(1)}, bf16[2,288,128]{2,1,0:T(8,128)(2,1)S(1)}, u32[]{:S(2)}, u32[]{:S(2)}) collective-permute-start(bf16[2,288,128]{2,1,0:T(8,128)(2,1)S(1)} %fusion.11), channel_id=1, source_target_pairs={{0,4},{1,5},{2,6},{3,7},{4,0},{5,1},{6,2},{7,3},{8,12},{9,13},{10,... | collective-permute-start | bytes 442376 | tf_op jit(solution)/shard_map/ppermute | solution.py:293
  142.7 5.7 %collective-permute-start.16 = (bf16[1,288,128]{2,1,0:T(8,128)(2,1)S(1)}, bf16[1,288,128]{2,1,0:T(8,128)(2,1)S(1)}, u32[]{:S(2)}, u32[]{:S(2)}) collective-permute-start(bf16[1,288,128]{2,1,0:T(8,128)(2,1)S(1)} %fusion.27), channel_id=1, source_target_pairs={{0,8},{1,9},{2,10},{3,11},{4,12},{5,13},{6,14},{7,15},{8,0},{9,1},... | collective-permute-start | bytes 221192 | tf_op jit(solution)/shard_map/ppermute | solution.py:293
  (20 other events, 186.9 us)

commit v2 on v1

--- a/solution.py
+++ b/solution.py
@@ -10,9 +10,10 @@
 
 
 LANES = 128
-CHUNKS = (2, 2, 2, 2)
+CHUNKS = (2, 3, 2, 1)
 BLOCKS = 4
 OUT_STEPS = 4
+PREP_MIB = 58
 
 
 def expert_block(arrived, held_up, held_down):
@@ -70,8 +71,12 @@
     return (moe_out, scales)
 
 
-def params(**kw):
-    return pltpu.CompilerParams(vmem_limit_bytes=58 * 1024 * 1024, **kw)
+def params(mib):
+    return pltpu.CompilerParams(vmem_limit_bytes=mib * 1024 * 1024)
+
+
+def flipped(slot, bits):
+    return sum(((slot >> b) & 1) << (bits - 1 - b) for b in range(bits))
 
 
 def vmem():
@@ -106,18 +111,18 @@
 def prep_kernel(me_ref, gate_ref, send_ref, keep_ref):
     rows, experts, cols = gate_ref.shape
     turned = gate_ref[...].reshape(rows * experts, cols).T
-    half = keep_ref.shape[2]
+    half = keep_ref.shape[1]
     parity = me_ref[0] % 2
     for d in range(cols // half):
         part = turned[d * half : (d + 1) * half]
 
         @pl.when(parity == d % 2)
         def _():
-            keep_ref[d // 2, 0] = part
+            keep_ref[d // 2] = part
 
         @pl.when(parity != d % 2)
         def _():
-            send_ref[d // 2, 0] = part
+            send_ref[d // 2] = part
 
 
 def max_kernel(w_ref, max_ref):
@@ -149,10 +154,10 @@
     return (rows == ids[k : k + 1]).astype(jnp.float32).astype(jnp.bfloat16)
 
 
-def hidden_kernel(first_k, per_k, top, experts, me_ref, got_ref, own_ref, pair_ref, *refs):
-    send_ref, keep_ref, own_x, pair_x = refs[-4:]
+def hidden_kernel(first_k, per_k, top, experts, bits, me_ref, got_ref, *refs):
+    weights, (send_ref, keep_ref, own_x, pair_x) = refs[:4], refs[4:]
     tokens = got_ref.shape[0]
-    blocks, rows, depth = own_ref.shape
+    blocks, half, depth = weights[0].shape
     width = depth // experts
     step = pl.program_id(0)
     me = me_ref[0]
@@ -173,24 +178,29 @@
                 )
 
     lanes = own_x.shape[2]
-    result = jnp.zeros((blocks * rows, lanes), jnp.float32)
-    for w_ref, x_ref in ((own_ref, own_x), (pair_ref, pair_x)):
+    result = jnp.zeros((2 * blocks * half, lanes), jnp.float32)
+    for at, x_ref in ((0, own_x), (2, pair_x)):
+        both = [w_ref[...].reshape(blocks * half, depth) for w_ref in weights[at : at + 2]]
         result = result + jnp.dot(
-            w_ref[...].reshape(blocks * rows, depth),
+            jnp.concatenate(both, axis=0),
             x_ref[...].reshape(depth, lanes),
             preferred_element_type=jnp.float32,
         )
+    count = send_ref.shape[0]
     for b in range(blocks):
-        part = result[b * rows : (b + 1) * rows]
-        slot = (step * blocks + b) ^ (me // 2)
-
-        @pl.when(slot % 2 == 0)
+        gate = result[b * half : (b + 1) * half]
+        up = result[(blocks + b) * half : (blocks + b + 1) * half]
+        place = flipped((step * blocks + b) ^ (me // 2), bits)
+
+        @pl.when(place < count)
         def _():
-            keep_ref[slot // 2] = part
-
-        @pl.when(slot % 2 != 0)
+            keep_ref[place, :half] = gate
+            keep_ref[place, half:] = up
+
+        @pl.when(place >= count)
         def _():
-            send_ref[slot // 2] = part.astype(jnp.bfloat16)
+            send_ref[place - count, :half] = gate.astype(jnp.bfloat16)
+            send_ref[place - count, half:] = up.astype(jnp.bfloat16)
 
 
 def left_terms(chunks, first_k, parts, top, experts, width, got_ref, pieces, left):
@@ -217,46 +227,35 @@
     refs[-1][...] = left_terms(chunks, 0, parts, top, experts, width, got_ref, refs[:-1], None)
 
 
-def down_kernel(chunk, first_k, parts, top, experts, base, *refs):
+def down_kernel(chunk, first_k, parts, top, experts, base, bits, *refs):
     me_ref, slot_ref, got_ref, before_ref, down_ref, scale_ref = refs[:6]
-    pieces = refs[6:-3]
-    send_ref, keep_ref, left_ref = refs[-3:]
+    pieces = refs[6:-5]
+    send_ref, keep_ref, left_ref, part_ref, expert_ref = refs[-5:]
     tokens = got_ref.shape[0]
     width = got_ref.shape[1] - LANES
 
     @pl.when(pl.program_id(0) == 0)
     def _():
+        for e in range(experts):
+            expert_ref[slot_ref[e]] = e
         left = left_terms(
             (chunk,), first_k, parts, top, experts, width, got_ref, pieces, before_ref[...]
         )
         left_ref[...] = left.reshape(-1, tokens).T
 
-    result = jnp.dot(left_ref[...], down_ref[...], preferred_element_type=jnp.float32)
+    part_ref[...] = jnp.dot(left_ref[...], down_ref[...], preferred_element_type=jnp.float32)
     me = me_ref[0]
     count = send_ref.shape[0]
     rows = tokens // (2 * count)
-    for d in range(2 * count):
-        slot = (d // 2) ^ (me // 2)
-
-        def put(out_ref):
-            for b in range(base // rows):
-                out_ref[slot, b * rows : (b + 1) * rows, :] = result[
-                    d * rows : (d + 1) * rows, b * LANES : (b + 1) * LANES
-                ]
-
-        pl.when(me % 2 == d % 2)(functools.partial(put, keep_ref))
-        pl.when(me % 2 != d % 2)(functools.partial(put, send_ref))
-
-    for e in range(experts):
-        slot = slot_ref[e] ^ me
-
-        @pl.when(slot % 2 == 0)
-        def _():
-            keep_ref[slot // 2, base:, :] = scale_ref[e, 0].astype(jnp.float32)
-
-        @pl.when(slot % 2 == 1)
-        def _():
-            send_ref[slot // 2, base:, :] = scale_ref[e, 0].astype(jnp.float32)
+    for place in range(2 * count):
+        out_ref = keep_ref if place < count else send_ref
+        d = flipped(place, bits) ^ me
+        at = pl.multiple_of(d * rows, rows)
+        for b in range(base // rows):
+            out_ref[place % count, b * rows : (b + 1) * rows, :] = part_ref[
+                pl.ds(at, rows), b * LANES : (b + 1) * LANES
+            ]
+        out_ref[place % count, base:, :] = scale_ref[expert_ref[d], 0].astype(jnp.float32)
 
 
 def finish_kernel(gate_cols, gate_factor, down_factor, base, extra, *refs):
@@ -286,13 +285,12 @@
     for stage, bits in enumerate(stages):
         count = 2**bits
         if stage:
-            split = [p.reshape((p.shape[0] // count, count) + p.shape[1:]) for p in pieces]
-            send = [merge([s[:, m] for s in split]) for m in range(1, count)]
-            pieces = [s[:, 0] for s in split]
+            size = pieces[0].shape[0] // count
+            send = [merge([p[m * size : (m + 1) * size] for p in pieces]) for m in range(1, count)]
+            pieces = [p[:size] for p in pieces]
         for m in range(1, count):
-            got = lax.ppermute(
-                send[m - 1], "ep", [(i, i ^ (m << shift)) for i in range(n)]
-            )
+            mask = flipped(m, bits) << shift
+            got = lax.ppermute(send[m - 1], "ep", [(i, i ^ mask) for i in range(n)])
             whole.append(got)
             pieces.append(got)
         shift += bits
@@ -316,7 +314,7 @@
         out_shape=jax.ShapeDtypeStruct((experts, cols), jnp.bfloat16),
         in_specs=[pl.BlockSpec((rows, experts, tile), lambda i: (0, 0, i))],
         out_specs=pl.BlockSpec((experts, tile), lambda i: (0, i)),
-        compiler_params=params(),
+        compiler_params=params(12),
         cost_estimate=pl.CostEstimate(
             flops=2 * w.size, bytes_accessed=2 * w.size, transcendentals=0
         ),
@@ -344,34 +342,36 @@
         out_shape=jax.ShapeDtypeStruct((n, tok_rows, 2 * gate_rows + LANES), jnp.bfloat16),
         in_specs=[vmem()] * 3,
         out_specs=vmem(),
-        compiler_params=params(),
+        compiler_params=params(62),
     )(tokens, expert_ids.T, gate_weights.T)
     got = lax.all_to_all(packed, "ep", split_axis=0, concat_axis=0, tiled=True)
     got = got.reshape(all_tokens, 2 * gate_rows + LANES)
 
     group = 8 if n % 8 == 0 else 4
     per_half = n // group
-    half_block = pl.BlockSpec(
-        (group // 2, 1, down_rows, depth), lambda i: (i % per_half, i // per_half, 0, 0)
-    )
-    half_shape = jax.ShapeDtypeStruct((n // 2, 2, down_rows, depth), jnp.bfloat16)
-    send, own = pl.pallas_call(
-        prep_kernel,
-        grid=(2 * per_half,),
-        out_shape=(half_shape,) * 2,
-        in_specs=[
-            smem(),
-            pl.BlockSpec((gate_rows, experts, group * down_rows), lambda i: (0, 0, i)),
-        ],
-        out_specs=(half_block,) * 2,
-        compiler_params=params(),
-        cost_estimate=pl.CostEstimate(
-            flops=2 * gate_up.size, bytes_accessed=4 * gate_up.size, transcendentals=0
-        ),
-    )(me, gate_up)
-    pair = lax.ppermute(send, "ep", [(i, i ^ 1) for i in range(n)])
-    own = own.reshape(n // 2, 2 * down_rows, depth)
-    pair = pair.reshape(n // 2, 2 * down_rows, depth)
+    block = pl.BlockSpec((group // 2, down_rows, depth), lambda i: (i, 0, 0))
+    half_shape = jax.ShapeDtypeStruct((n // 2, down_rows, depth), jnp.bfloat16)
+    own, pair = [], []
+    for half in range(2):
+        send, keep = pl.pallas_call(
+            prep_kernel,
+            grid=(per_half,),
+            out_shape=(half_shape,) * 2,
+            in_specs=[
+                smem(),
+                pl.BlockSpec(
+                    (gate_rows, experts, group * down_rows),
+                    lambda i, half=half: (0, 0, half * per_half + i),
+                ),
+            ],
+            out_specs=(block,) * 2,
+            compiler_params=params(PREP_MIB),
+            cost_estimate=pl.CostEstimate(
+                flops=gate_up.size, bytes_accessed=2 * gate_up.size, transcendentals=0
+            ),
+        )(me, gate_up)
+        pair.append(lax.ppermute(send, "ep", [(i, i ^ 1) for i in range(n)]))
+        own.append(keep)
 
     blocks = BLOCKS if (n // 2) % BLOCKS == 0 else 2
     all_pieces, first_k = [], 0
@@ -379,23 +379,23 @@
         lanes = per_k * all_tokens
         shape = (n // 4, 2 * down_rows, lanes)
         send, keep = pl.pallas_call(
-            functools.partial(hidden_kernel, first_k, per_k, top, experts),
+            functools.partial(hidden_kernel, first_k, per_k, top, experts, bits - 1),
             grid=(n // 2 // blocks,),
             out_shape=(
                 jax.ShapeDtypeStruct(shape, jnp.bfloat16),
                 jax.ShapeDtypeStruct(shape, jnp.float32),
             ),
             in_specs=[smem(), vmem()]
-            + [pl.BlockSpec((blocks, 2 * down_rows, depth), lambda i: (i, 0, 0))] * 2,
+            + [pl.BlockSpec((blocks, down_rows, depth), lambda i: (i, 0, 0))] * 4,
             out_specs=(pl.BlockSpec(shape, lambda i: (0, 0, 0)),) * 2,
             scratch_shapes=[pltpu.VMEM((gate_rows, experts, lanes), jnp.bfloat16)] * 2,
-            compiler_params=params(),
+            compiler_params=params(34),
             cost_estimate=pl.CostEstimate(
                 flops=2 * depth * gate_cols * lanes,
                 bytes_accessed=2 * depth * gate_cols + 3 * gate_cols * lanes // 2,
                 transcendentals=0,
             ),
-        )(me, got, own, pair)
+        )(me, got, *own, *pair)
         first_k += per_k
         all_pieces += scatter([send], keep, n, 1, HIDDEN_STAGES(bits - 1), add_up)
 
@@ -422,13 +422,13 @@
         out_shape=jax.ShapeDtypeStruct((down_rows, experts, all_tokens), jnp.bfloat16),
         in_specs=[vmem()] + [first_slot(p) for p in early],
         out_specs=vmem(),
-        compiler_params=params(),
+        compiler_params=params(16),
     )(got, *early)
     shape = (n // 2, steps * (base + extra), LANES)
     out_block = pl.BlockSpec((n // 2, base + extra, LANES), lambda i: (0, i, 0))
     send, keep = pl.pallas_call(
         functools.partial(
-            down_kernel, chunks[-1], top - chunks[-1], parts, top, experts, base
+            down_kernel, chunks[-1], top - chunks[-1], parts, top, experts, base, bits
         ),
         grid=(steps,),
         out_shape=(jax.ShapeDtypeStruct(shape, jnp.float32),) * 2,
@@ -442,8 +442,12 @@
         ]
         + [first_slot(p) for p in late],
         out_specs=(out_block,) * 2,
-        scratch_shapes=[pltpu.VMEM((all_tokens, down_rows * experts), jnp.bfloat16)],
-        compiler_params=params(),
+        scratch_shapes=[
+            pltpu.VMEM((all_tokens, down_rows * experts), jnp.bfloat16),
+            pltpu.VMEM((all_tokens, model_width // steps), jnp.float32),
+            pltpu.SMEM((n,), jnp.int32),
+        ],
+        compiler_params=params(20),
     )(
         me,
         owner_slot,
@@ -478,7 +482,7 @@
         ),
         in_specs=[first_slot(p) for p in pieces],
         out_specs=(vmem(),) * 2,
-        compiler_params=params(),
+        compiler_params=params(8),
     )(*pieces)
 
 

time: 151 us -> 121 us (0.80)
  Pallas kernels: 56.9 us -> 38.3 us
  waiting for transfers between devices: 63.4 us -> 50.8 us
    ppermute x17 -> x18, waiting for transfers between devices: 60.7 us -> 47.9 us  [the longest x16 47.9 us: scatter(): got = lax.ppermute(send[m - 1], 'ep', [(i, i ^ mask) for i in range(n)])]
    pallas_call x4, Pallas kernels: 30.2 us -> 22.9 us  [row_path(): pl.pallas_call(functools.partial(hidden_kernel, first_k, per_k, top, expe...]
    pallas_call x2, Pallas kernels: 6.27 us -> 1.34 us  [column_max(): pl.pallas_call(max_kernel, grid=(parts,), out_shape=jax.ShapeDtypeStruct(...]
    pallas_call x1, Pallas kernels: 6.84 us -> 3.09 us  [row_path(): pl.pallas_call(functools.partial(down_kernel, chunks[-1], top - chunks[-1...]
    unnamed x53 -> x13, local copies, waits for them, and re-layouts: 3.32 us -> 6.96 us
    pallas_call x1, Pallas kernels: 3.13 us -> 1 us  [row_path(): pl.pallas_call(functools.partial(left_kernel, chunks[:-1], parts, top, ex...]
    ppermute x17 -> x18, starting transfers between devices: 14.4 us -> 15 us  [the longest x16 14.5 us: scatter(): got = lax.ppermute(send[m - 1], 'ep', [(i, i ^ mask) for i in range(n)])]
    pallas_call x1 -> x2, Pallas kernels: 7.04 us -> 7.62 us  [row_path(): pl.pallas_call(prep_kernel, grid=(per_half,), out_shape=(half_shape,) * 2...]
  transfers between devices with their start and end apart: 18 -> 19, of which waited for: 13 -> 8; matrix products, arithmetic and copies ran while one was open for 2% -> 0% of each run, Pallas kernels for 7% -> 22%
where the time goes in v2:
time: 121 us; the launch traced here: 120 us
  waiting for transfers between devices  50.8 us (42%)
  Pallas kernels  38.3 us (32%)
  starting transfers between devices  22.4 us (19%)
  local copies, waits for them, and re-layouts  6.97 us (6%)
    ppermute x16, waiting for transfers between devices, scatter(): got = lax.ppermute(send[m - 1], 'ep', [(i, i ^ mask) for i in range(n)])  47.9 us
    pallas_call x4, Pallas kernels, row_path(): pl.pallas_call(functools.partial(hidden_kernel, first_k, per_k, top, expe...  22.9 us
    ppermute x16, starting transfers between devices, scatter(): got = lax.ppermute(send[m - 1], 'ep', [(i, i ^ mask) for i in range(n)])  14.5 us
    pallas_call x2, Pallas kernels, row_path(): pl.pallas_call(prep_kernel, grid=(per_half,), out_shape=(half_shape,) * 2...  7.62 us
    all_to_all x1, starting transfers between devices, row_path(): got = lax.all_to_all(packed, 'ep', split_axis=0, concat_axis=0, tiled=True)  7.39 us
    unnamed x13, local copies, waits for them, and re-layouts  6.96 us
    pallas_call x1, Pallas kernels, row_path(): pl.pallas_call(functools.partial(down_kernel, chunks[-1], top - chunks[-1...  3.09 us
    all_to_all x1, waiting for transfers between devices, row_path(): got = lax.all_to_all(packed, 'ep', split_axis=0, concat_axis=0, tiled=True)  2.89 us
  transfers between devices with their start and end apart: 19, of which 8 were waited for; matrix products, arithmetic and copies ran while one was open for 0% of the time, Pallas kernels for 22%

profile of v2, /device:TPU:0, one launch (start us, length us, event | category | flops | bytes accessed | tf_op | source)
XLA Modules:
  0.0 120.3 jit_solution(16162203178368554403)
XLA Ops:
  0.6 3.8 %shard_map.78 = (bf16[8,48,2048]{2,1,0:T(8,128)(2,1)}, bf16[8,48,2048]{2,1,0:T(8,128)(2,1)}) custom-call(s32[1]{0:T(128)} %bitcast.me_ref.refs_0_, bf16[128,16,1536]{2,1,0:T(8,128)(2,1)} %w_ref.2), custom_call_target="tpu_custom_call" | custom-call | flops 3145728 | bytes 6291456 | tf_op jit(solution)/shard_map/pallas_call | solution.py:356
  4.9 3.8 %shard_map.79 = (bf16[8,48,2048]{2,1,0:T(8,128)(2,1)}, bf16[8,48,2048]{2,1,0:T(8,128)(2,1)}) custom-call(s32[1]{0:T(128)} %bitcast.me_ref.refs_0_, bf16[128,16,1536]{2,1,0:T(8,128)(2,1)} %w_ref.2), custom_call_target="tpu_custom_call" | custom-call | flops 3145728 | bytes 6291456 | tf_op jit(solution)/shard_map/pallas_call | solution.py:356
  8.8 1.6 %shard_map.77 = bf16[16,16,384]{2,1,0:T(8,128)(2,1)} custom-call(bf16[16,2048]{1,0:T(8,128)(2,1)} %tok_ref.1, s32[8,16]{1,0:T(8,128)} %bitcast.17, f32[8,16]{1,0:T(8,128)} %bitcast.18), custom_call_target="tpu_custom_call" | custom-call | tf_op jit(solution)/shard_map/pallas_call | solution.py:340
  10.4 7.4 %all-to-all-start = ((bf16[16,16,384]{2,1,0:T(8,128)(2,1)}), bf16[16,16,384]{2,1,0:T(8,128)(2,1)S(1)}, u32[]{:S(2)}, u32[]{:S(2)}) async-start(bf16[16,16,384]{2,1,0:T(8,128)(2,1)} %shard_map.77), calls=%async_computation | async-start | bytes 393216 | tf_op jit(solution)/shard_map/all_to_all | solution.py:347
  17.8 1.9 %copy-done.1 = bf16[48,16,2048]{2,1,0:T(8,128)(2,1)S(1)} copy-done((bf16[48,16,2048]{2,1,0:T(8,128)(2,1)S(1)}, bf16[48,16,2048]{2,1,0:T(8,128)(2,1)}, u32[]{:S(2)}) %copy-start.1) | copy-done | bytes 3145752
  20.2 2.8 %copy-done = bf16[128,16,1536]{2,1,0:T(8,128)(2,1)S(1)} copy-done((bf16[128,16,1536]{2,1,0:T(8,128)(2,1)S(1)}, bf16[128,16,1536]{2,1,0:T(8,128)(2,1)}, u32[]{:S(2)}) %copy-start) | copy-done | bytes 6291480
  23.8 2.9 %all-to-all-done = bf16[16,16,384]{2,1,0:T(8,128)(2,1)S(1)} async-done(((bf16[16,16,384]{2,1,0:T(8,128)(2,1)}), bf16[16,16,384]{2,1,0:T(8,128)(2,1)S(1)}, u32[]{:S(2)}, u32[]{:S(2)}) %all-to-all-start) | async-done | bytes 196640 | tf_op jit(solution)/shard_map/all_to_all | solution.py:347
  26.8 1.4 %copy-done.4 = bf16[8,48,2048]{2,1,0:T(8,128)(2,1)S(1)} copy-done((bf16[8,48,2048]{2,1,0:T(8,128)(2,1)S(1)}, bf16[8,48,2048]{2,1,0:T(8,128)(2,1)}, u32[]{:S(2)}) %copy-start.4) | copy-done | bytes 1572888
  28.2 4.1 %shard_map.86 = (bf16[4,96,256]{2,1,0:T(8,128)(2,1)S(1)}, f32[4,96,256]{2,1,0:T(8,128)S(1)}) custom-call(s32[1]{0:T(128)} %bitcast.me_ref.refs_0_, bf16[256,384]{1,0:T(8,128)(2,1)S(1)} %bitcast.10, bf16[8,48,2048]{2,1,0:T(8,128)(2,1)S(1)} %copy-done.3, bf16[8,48,2048]{2,1,0:T(8,128)(2,1)S(1)} %copy-done.4, ...), custom_call_target="tpu_custom_call" | custom-call | flops 1610612736 | bytes 6881280 | tf_op jit(solution)/shard_map/pallas_call | solution.py:381
  32.3 5.7 %shard_map.82 = (bf16[4,96,512]{2,1,0:T(8,128)(2,1)S(1)}, f32[4,96,512]{2,1,0:T(8,128)S(1)}) custom-call(s32[1]{0:T(128)} %bitcast.me_ref.refs_0_, bf16[256,384]{1,0:T(8,128)(2,1)S(1)} %bitcast.11, bf16[8,48,2048]{2,1,0:T(8,128)(2,1)S(1)} %copy-done.3, bf16[8,48,2048]{2,1,0:T(8,128)(2,1)S(1)} %copy-done.4, ...), custom_call_target="tpu_custom_call" | custom-call | flops 3221225472 | bytes 7471104 | tf_op jit(solution)/shard_map/pallas_call | solution.py:381
  38.0 2.1 %collective-permute-start.8 = (bf16[4,96,512]{2,1,0:T(8,128)(2,1)S(1)}, bf16[4,96,512]{2,1,0:T(8,128)(2,1)S(1)}, u32[]{:S(2)}, u32[]{:S(2)}) collective-permute-start(bf16[4,96,512]{2,1,0:T(8,128)(2,1)S(1)} %get-tuple-element.25), channel_id=1, source_target_pairs={{0,2},{1,3},{2,0},{3,1},{4,6},{5,7},{6,4},{7,5},{8,10},{9,11},{10,... | collective-permute-start | bytes 1179656 | tf_op jit(solution)/shard_map/ppermute | solution.py:293
  40.1 5.7 %shard_map.80 = (bf16[4,96,512]{2,1,0:T(8,128)(2,1)S(1)}, f32[4,96,512]{2,1,0:T(8,128)S(1)}) custom-call(s32[1]{0:T(128)} %bitcast.me_ref.refs_0_, bf16[256,384]{1,0:T(8,128)(2,1)S(1)} %bitcast.12, bf16[8,48,2048]{2,1,0:T(8,128)(2,1)S(1)} %copy-done.3, bf16[8,48,2048]{2,1,0:T(8,128)(2,1)S(1)} %copy-done.4, ...), custom_call_target="tpu_custom_call" | custom-call | flops 3221225472 | bytes 7471104 | tf_op jit(solution)/shard_map/pallas_call | solution.py:381
  47.0 7.4 %shard_map.81 = (bf16[4,96,768]{2,1,0:T(8,128)(2,1)S(1)}, f32[4,96,768]{2,1,0:T(8,128)S(1)}) custom-call(s32[1]{0:T(128)} %bitcast.me_ref.refs_0_, bf16[256,384]{1,0:T(8,128)(2,1)S(1)} %bitcast.13, bf16[8,48,2048]{2,1,0:T(8,128)(2,1)S(1)} %copy-done.3, bf16[8,48,2048]{2,1,0:T(8,128)(2,1)S(1)} %copy-done.4, ...), custom_call_target="tpu_custom_call" | custom-call | flops 4831838208 | bytes 8060928 | tf_op jit(solution)/shard_map/pallas_call | solution.py:381
  55.6 1.9 %collective-permute-start.13 = (bf16[1,96,256]{2,1,0:T(8,128)(2,1)S(1)}, bf16[1,96,256]{2,1,0:T(8,128)(2,1)S(1)}, u32[]{:S(2)}, u32[]{:S(2)}) collective-permute-start(bf16[1,96,256]{2,1,0:T(8,128)(2,1)S(1)} %add_convert_fusion.7), channel_id=1, source_target_pairs={{0,8},{1,9},{2,10},{3,11},{4,12},{5,13},{6,14},{7,15},{8,0},{9,1},... | collective-permute-start | bytes 147464 | tf_op jit(solution)/shard_map/ppermute | solution.py:293
  58.6 1.2 %collective-permute-start.3 = (bf16[2,96,512]{2,1,0:T(8,128)(2,1)S(1)}, bf16[2,96,512]{2,1,0:T(8,128)(2,1)S(1)}, u32[]{:S(2)}, u32[]{:S(2)}) collective-permute-start(bf16[2,96,512]{2,1,0:T(8,128)(2,1)S(1)} %add_convert_fusion.2), channel_id=1, source_target_pairs={{0,4},{1,5},{2,6},{3,7},{4,0},{5,1},{6,2},{7,3},{8,12},{9,13},{10,... | collective-permute-start | bytes 589832 | tf_op jit(solution)/shard_map/ppermute | solution.py:293
  59.8 10.4 %collective-permute-done.5.refs_5_ = bf16[4,96,768]{2,1,0:T(8,128)(2,1)S(1)} collective-permute-done((bf16[4,96,768]{2,1,0:T(8,128)(2,1)S(1)}, bf16[4,96,768]{2,1,0:T(8,128)(2,1)S(1)}, u32[]{:S(2)}, u32[]{:S(2)}) %collective-permute-start.5) | collective-permute-done | bytes 589856 | tf_op jit(solution)/shard_map/ppermute | solution.py:293
  71.2 2.4 %collective-permute-start.10 = (bf16[1,96,512]{2,1,0:T(8,128)(2,1)S(1)}, bf16[1,96,512]{2,1,0:T(8,128)(2,1)S(1)}, u32[]{:S(2)}, u32[]{:S(2)}) collective-permute-start(bf16[1,96,512]{2,1,0:T(8,128)(2,1)S(1)} %add_convert_fusion.5), channel_id=1, source_target_pairs={{0,8},{1,9},{2,10},{3,11},{4,12},{5,13},{6,14},{7,15},{8,0},{9,1},... | collective-permute-start | bytes 294920 | tf_op jit(solution)/shard_map/ppermute | solution.py:293
  74.3 8.3 %collective-permute-done.6.refs_6_ = bf16[2,96,768]{2,1,0:T(8,128)(2,1)S(1)} collective-permute-done((bf16[2,96,768]{2,1,0:T(8,128)(2,1)S(1)}, bf16[2,96,768]{2,1,0:T(8,128)(2,1)S(1)}, u32[]{:S(2)}, u32[]{:S(2)}) %collective-permute-start.6) | collective-permute-done | bytes 294944 | tf_op jit(solution)/shard_map/ppermute | solution.py:293
  83.3 7.7 %collective-permute-done.7.refs_7_ = bf16[1,96,768]{2,1,0:T(8,128)(2,1)S(1)} collective-permute-done((bf16[1,96,768]{2,1,0:T(8,128)(2,1)S(1)}, bf16[1,96,768]{2,1,0:T(8,128)(2,1)S(1)}, u32[]{:S(2)}, u32[]{:S(2)}) %collective-permute-start.7) | collective-permute-done | bytes 147488 | tf_op jit(solution)/shard_map/ppermute | solution.py:293
  92.9 3.1 %shard_map.87 = (f32[8,288,128]{2,1,0:T(8,128)S(1)}, f32[8,288,128]{2,1,0:T(8,128)S(1)}) custom-call(s32[1]{0:T(128)} %bitcast.me_ref.refs_0_, s32[16]{0:T(128)S(1)} %copy-done.5, bf16[256,384]{1,0:T(8,128)(2,1)S(1)} %bitcast.15, bf16[48,16,256]{2,1,0:T(8,128)(2,1)S(1)} %shard_map.83.refs_3_, bf16[768,2048]{1,0:T(8,128)(2,1)S(1)} %bitcast.9, ...), custom_call_target="tpu_custom_call" | custom-call | tf_op jit(solution)/shard_map/pallas_call | solution.py:429
  96.1 2.8 %collective-permute-done.14.refs_1_ = f32[8,288,128]{2,1,0:T(8,128)S(1)} collective-permute-done((f32[8,288,128]{2,1,0:T(8,128)S(1)}, f32[8,288,128]{2,1,0:T(8,128)S(1)}, u32[]{:S(2)}, u32[]{:S(2)}) %collective-permute-start.14) | collective-permute-done | bytes 1179680 | tf_op jit(solution)/shard_map/ppermute | solution.py:293
  100.0 8.4 %collective-permute-done.15.refs_2_ = bf16[4,288,128]{2,1,0:T(8,128)(2,1)S(1)} collective-permute-done((bf16[4,288,128]{2,1,0:T(8,128)(2,1)S(1)}, bf16[4,288,128]{2,1,0:T(8,128)(2,1)S(1)}, u32[]{:S(2)}, u32[]{:S(2)}) %collective-permute-start.15) | collective-permute-done | bytes 294944 | tf_op jit(solution)/shard_map/ppermute | solution.py:293
  108.6 5.1 %collective-permute-done.16.refs_3_ = bf16[2,288,128]{2,1,0:T(8,128)(2,1)S(1)} collective-permute-done((bf16[2,288,128]{2,1,0:T(8,128)(2,1)S(1)}, bf16[2,288,128]{2,1,0:T(8,128)(2,1)S(1)}, u32[]{:S(2)}, u32[]{:S(2)}) %collective-permute-start.16) | collective-permute-done | bytes 147488 | tf_op jit(solution)/shard_map/ppermute | solution.py:293
  114.4 5.2 %collective-permute-done.17.refs_4_ = bf16[1,288,128]{2,1,0:T(8,128)(2,1)S(1)} collective-permute-done((bf16[1,288,128]{2,1,0:T(8,128)(2,1)S(1)}, bf16[1,288,128]{2,1,0:T(8,128)(2,1)S(1)}, u32[]{:S(2)}, u32[]{:S(2)}) %collective-permute-start.17) | collective-permute-done | bytes 73760 | tf_op jit(solution)/shard_map/ppermute | solution.py:293
  (55 shorter events, 12.4 us)
Async XLA Ops:
  4.4 22.3 %collective-permute-start = (bf16[8,48,2048]{2,1,0:T(8,128)(2,1)}, bf16[8,48,2048]{2,1,0:T(8,128)(2,1)S(1)}, u32[]{:S(2)}, u32[]{:S(2)}) collective-permute-start(bf16[8,48,2048]{2,1,0:T(8,128)(2,1)} %get-tuple-element.18), channel_id=1, source_target_pairs={{0,1},{1,0},{2,3},{3,2},{4,5},{5,4},{6,7},{7,6},{8,9},{9,8},{10,11... | collective-permute-start | bytes 4718600 | tf_op jit(solution)/shard_map/ppermute | solution.py:373
  8.8 18.0 %collective-permute-start.1 = (bf16[8,48,2048]{2,1,0:T(8,128)(2,1)}, bf16[8,48,2048]{2,1,0:T(8,128)(2,1)}, u32[]{:S(2)}, u32[]{:S(2)}) collective-permute-start(bf16[8,48,2048]{2,1,0:T(8,128)(2,1)} %get-tuple-element.19), channel_id=1, source_target_pairs={{0,1},{1,0},{2,3},{3,2},{4,5},{5,4},{6,7},{7,6},{8,9},{9,8},{10,11... | collective-permute-start | bytes 4718600 | tf_op jit(solution)/shard_map/ppermute | solution.py:373
  10.4 16.4 %all-to-all-start = ((bf16[16,16,384]{2,1,0:T(8,128)(2,1)}), bf16[16,16,384]{2,1,0:T(8,128)(2,1)S(1)}, u32[]{:S(2)}, u32[]{:S(2)}) async-start(bf16[16,16,384]{2,1,0:T(8,128)(2,1)} %shard_map.77), calls=%async_computation | async-start | bytes 393216 | tf_op jit(solution)/shard_map/all_to_all | solution.py:347
  17.8 1.9 %copy-start.1 = (bf16[48,16,2048]{2,1,0:T(8,128)(2,1)S(1)}, bf16[48,16,2048]{2,1,0:T(8,128)(2,1)}, u32[]{:S(2)}) copy-start(bf16[48,16,2048]{2,1,0:T(8,128)(2,1)} %w_ref.3) | copy-start | bytes 9437188
  20.1 2.8 %copy-start = (bf16[128,16,1536]{2,1,0:T(8,128)(2,1)S(1)}, bf16[128,16,1536]{2,1,0:T(8,128)(2,1)}, u32[]{:S(2)}) copy-start(bf16[128,16,1536]{2,1,0:T(8,128)(2,1)} %w_ref.2) | copy-start | bytes 18874372
  22.9 3.8 %copy-start.3 = (bf16[8,48,2048]{2,1,0:T(8,128)(2,1)S(1)}, bf16[8,48,2048]{2,1,0:T(8,128)(2,1)}, u32[]{:S(2)}) copy-start(bf16[8,48,2048]{2,1,0:T(8,128)(2,1)} %get-tuple-element.16.refs_0_) | copy-start | bytes 4718596
  32.2 13.8 %collective-permute-start.11 = (bf16[4,96,256]{2,1,0:T(8,128)(2,1)S(1)}, bf16[4,96,256]{2,1,0:T(8,128)(2,1)S(1)}, u32[]{:S(2)}, u32[]{:S(2)}) collective-permute-start(bf16[4,96,256]{2,1,0:T(8,128)(2,1)S(1)} %get-tuple-element.27), channel_id=1, source_target_pairs={{0,2},{1,3},{2,0},{3,1},{4,6},{5,7},{6,4},{7,5},{8,10},{9,11},{10,... | collective-permute-start | bytes 589832 | tf_op jit(solution)/shard_map/ppermute | solution.py:293
  38.0 19.5 %collective-permute-start.8 = (bf16[4,96,512]{2,1,0:T(8,128)(2,1)S(1)}, bf16[4,96,512]{2,1,0:T(8,128)(2,1)S(1)}, u32[]{:S(2)}, u32[]{:S(2)}) collective-permute-start(bf16[4,96,512]{2,1,0:T(8,128)(2,1)S(1)} %get-tuple-element.25), channel_id=1, source_target_pairs={{0,2},{1,3},{2,0},{3,1},{4,6},{5,7},{6,4},{7,5},{8,10},{9,11},{10,... | collective-permute-start | bytes 1179656 | tf_op jit(solution)/shard_map/ppermute | solution.py:293
  45.9 12.7 %collective-permute-start.2 = (bf16[4,96,512]{2,1,0:T(8,128)(2,1)S(1)}, bf16[4,96,512]{2,1,0:T(8,128)(2,1)S(1)}, u32[]{:S(2)}, u32[]{:S(2)}) collective-permute-start(bf16[4,96,512]{2,1,0:T(8,128)(2,1)S(1)} %get-tuple-element.21), channel_id=1, source_target_pairs={{0,2},{1,3},{2,0},{3,1},{4,6},{5,7},{6,4},{7,5},{8,10},{9,11},{10,... | collective-permute-start | bytes 1179656 | tf_op jit(solution)/shard_map/ppermute | solution.py:293
  46.0 9.6 %collective-permute-start.12 = (bf16[2,96,256]{2,1,0:T(8,128)(2,1)S(1)}, bf16[2,96,256]{2,1,0:T(8,128)(2,1)S(1)}, u32[]{:S(2)}, u32[]{:S(2)}) collective-permute-start(bf16[2,96,256]{2,1,0:T(8,128)(2,1)S(1)} %add_convert_fusion.4), channel_id=1, source_target_pairs={{0,4},{1,5},{2,6},{3,7},{4,0},{5,1},{6,2},{7,3},{8,12},{9,13},{10,... | collective-permute-start | bytes 294920 | tf_op jit(solution)/shard_map/ppermute | solution.py:293
  54.4 15.7 %collective-permute-start.5 = (bf16[4,96,768]{2,1,0:T(8,128)(2,1)S(1)}, bf16[4,96,768]{2,1,0:T(8,128)(2,1)S(1)}, u32[]{:S(2)}, u32[]{:S(2)}) collective-permute-start(bf16[4,96,768]{2,1,0:T(8,128)(2,1)S(1)} %get-tuple-element.23), channel_id=1, source_target_pairs={{0,2},{1,3},{2,0},{3,1},{4,6},{5,7},{6,4},{7,5},{8,10},{9,11},{10,... | collective-permute-start | bytes 1769480 | tf_op jit(solution)/shard_map/ppermute | solution.py:293
  55.6 36.4 %collective-permute-start.13 = (bf16[1,96,256]{2,1,0:T(8,128)(2,1)S(1)}, bf16[1,96,256]{2,1,0:T(8,128)(2,1)S(1)}, u32[]{:S(2)}, u32[]{:S(2)}) collective-permute-start(bf16[1,96,256]{2,1,0:T(8,128)(2,1)S(1)} %add_convert_fusion.7), channel_id=1, source_target_pairs={{0,8},{1,9},{2,10},{3,11},{4,12},{5,13},{6,14},{7,15},{8,0},{9,1},... | collective-permute-start | bytes 147464 | tf_op jit(solution)/shard_map/ppermute | solution.py:293
  57.6 13.6 %collective-permute-start.9 = (bf16[2,96,512]{2,1,0:T(8,128)(2,1)S(1)}, bf16[2,96,512]{2,1,0:T(8,128)(2,1)S(1)}, u32[]{:S(2)}, u32[]{:S(2)}) collective-permute-start(bf16[2,96,512]{2,1,0:T(8,128)(2,1)S(1)} %add_convert_fusion.1), channel_id=1, source_target_pairs={{0,4},{1,5},{2,6},{3,7},{4,0},{5,1},{6,2},{7,3},{8,12},{9,13},{10,... | collective-permute-start | bytes 589832 | tf_op jit(solution)/shard_map/ppermute | solution.py:293
  58.6 15.0 %collective-permute-start.3 = (bf16[2,96,512]{2,1,0:T(8,128)(2,1)S(1)}, bf16[2,96,512]{2,1,0:T(8,128)(2,1)S(1)}, u32[]{:S(2)}, u32[]{:S(2)}) collective-permute-start(bf16[2,96,512]{2,1,0:T(8,128)(2,1)S(1)} %add_convert_fusion.2), channel_id=1, source_target_pairs={{0,4},{1,5},{2,6},{3,7},{4,0},{5,1},{6,2},{7,3},{8,12},{9,13},{10,... | collective-permute-start | bytes 589832 | tf_op jit(solution)/shard_map/ppermute | solution.py:293
  70.2 12.3 %collective-permute-start.6 = (bf16[2,96,768]{2,1,0:T(8,128)(2,1)S(1)}, bf16[2,96,768]{2,1,0:T(8,128)(2,1)S(1)}, u32[]{:S(2)}, u32[]{:S(2)}) collective-permute-start(bf16[2,96,768]{2,1,0:T(8,128)(2,1)S(1)} %add_convert_fusion), channel_id=1, source_target_pairs={{0,4},{1,5},{2,6},{3,7},{4,0},{5,1},{6,2},{7,3},{8,12},{9,13},{10,... | collective-permute-start | bytes 884744 | tf_op jit(solution)/shard_map/ppermute | solution.py:293
  71.2 12.1 %collective-permute-start.10 = (bf16[1,96,512]{2,1,0:T(8,128)(2,1)S(1)}, bf16[1,96,512]{2,1,0:T(8,128)(2,1)S(1)}, u32[]{:S(2)}, u32[]{:S(2)}) collective-permute-start(bf16[1,96,512]{2,1,0:T(8,128)(2,1)S(1)} %add_convert_fusion.5), channel_id=1, source_target_pairs={{0,8},{1,9},{2,10},{3,11},{4,12},{5,13},{6,14},{7,15},{8,0},{9,1},... | collective-permute-start | bytes 294920 | tf_op jit(solution)/shard_map/ppermute | solution.py:293
  73.6 9.7 %collective-permute-start.4 = (bf16[1,96,512]{2,1,0:T(8,128)(2,1)S(1)}, bf16[1,96,512]{2,1,0:T(8,128)(2,1)S(1)}, u32[]{:S(2)}, u32[]{:S(2)}) collective-permute-start(bf16[1,96,512]{2,1,0:T(8,128)(2,1)S(1)} %add_convert_fusion.6), channel_id=1, source_target_pairs={{0,8},{1,9},{2,10},{3,11},{4,12},{5,13},{6,14},{7,15},{8,0},{9,1},... | collective-permute-start | bytes 294920 | tf_op jit(solution)/shard_map/ppermute | solution.py:293
  82.6 8.4 %collective-permute-start.7 = (bf16[1,96,768]{2,1,0:T(8,128)(2,1)S(1)}, bf16[1,96,768]{2,1,0:T(8,128)(2,1)S(1)}, u32[]{:S(2)}, u32[]{:S(2)}) collective-permute-start(bf16[1,96,768]{2,1,0:T(8,128)(2,1)S(1)} %add_convert_fusion.3), channel_id=1, source_target_pairs={{0,8},{1,9},{2,10},{3,11},{4,12},{5,13},{6,14},{7,15},{8,0},{9,1},... | collective-permute-start | bytes 442376 | tf_op jit(solution)/shard_map/ppermute | solution.py:293
  83.3 8.7 %copy-start.5 = (s32[16]{0:T(128)S(1)}, s32[16]{0:T(128)}, u32[]{:S(2)}) copy-start(s32[16]{0:T(128)} %refs_1_.1) | copy-start | bytes 196
  91.0 1.9 %copy-start.2 = (bf16[48,16,2048]{2,1,0:T(8,128)(2,1)S(1)}, bf16[48,16,2048]{2,1,0:T(8,128)(2,1)}, u32[]{:S(2)}) copy-start(bf16[48,16,2048]{2,1,0:T(8,128)(2,1)} %w_ref.3) | copy-start | bytes 9437188
  96.0 2.9 %collective-permute-start.14 = (f32[8,288,128]{2,1,0:T(8,128)S(1)}, f32[8,288,128]{2,1,0:T(8,128)S(1)}, u32[]{:S(2)}, u32[]{:S(2)}) collective-permute-start(f32[8,288,128]{2,1,0:T(8,128)S(1)} %get-tuple-element.29), channel_id=1, source_target_pairs={{0,1},{1,0},{2,3},{3,2},{4,5},{5,4},{6,7},{7,6},{8,9},{9,8},{10,11... | collective-permute-start | bytes 3538952 | tf_op jit(solution)/shard_map/ppermute | solution.py:293
  99.2 9.1 %collective-permute-start.15 = (bf16[4,288,128]{2,1,0:T(8,128)(2,1)S(1)}, bf16[4,288,128]{2,1,0:T(8,128)(2,1)S(1)}, u32[]{:S(2)}, u32[]{:S(2)}) collective-permute-start(bf16[4,288,128]{2,1,0:T(8,128)(2,1)S(1)} %select_convert_fusion), channel_id=1, source_target_pairs={{0,2},{1,3},{2,0},{3,1},{4,6},{5,7},{6,4},{7,5},{8,10},{9,11},{10,... | collective-permute-start | bytes 884744 | tf_op jit(solution)/shard_map/ppermute | solution.py:293
  108.5 5.2 %collective-permute-start.16 = (bf16[2,288,128]{2,1,0:T(8,128)(2,1)S(1)}, bf16[2,288,128]{2,1,0:T(8,128)(2,1)S(1)}, u32[]{:S(2)}, u32[]{:S(2)}) collective-permute-start(bf16[2,288,128]{2,1,0:T(8,128)(2,1)S(1)} %fusion.1), channel_id=1, source_target_pairs={{0,4},{1,5},{2,6},{3,7},{4,0},{5,1},{6,2},{7,3},{8,12},{9,13},{10,... | collective-permute-start | bytes 442376 | tf_op jit(solution)/shard_map/ppermute | solution.py:293
  113.9 5.7 %collective-permute-start.17 = (bf16[1,288,128]{2,1,0:T(8,128)(2,1)S(1)}, bf16[1,288,128]{2,1,0:T(8,128)(2,1)S(1)}, u32[]{:S(2)}, u32[]{:S(2)}) collective-permute-start(bf16[1,288,128]{2,1,0:T(8,128)(2,1)S(1)} %fusion.3), channel_id=1, source_target_pairs={{0,8},{1,9},{2,10},{3,11},{4,12},{5,13},{6,14},{7,15},{8,0},{9,1},... | collective-permute-start | bytes 221192 | tf_op jit(solution)/shard_map/ppermute | solution.py:293
  (1 other events, 1.4 us)

commit v3 on v2

--- a/solution.py
+++ b/solution.py
@@ -10,7 +10,7 @@
 
 
 LANES = 128
-CHUNKS = (2, 3, 2, 1)
+CHUNKS = ((2, 0), (3, 0), (1, 1), (2, 0))
 BLOCKS = 4
 OUT_STEPS = 4
 PREP_MIB = 58
@@ -75,8 +75,18 @@
     return pltpu.CompilerParams(vmem_limit_bytes=mib * 1024 * 1024)
 
 
-def flipped(slot, bits):
-    return sum(((slot >> b) & 1) << (bits - 1 - b) for b in range(bits))
+def bit_order(bits, turn):
+    return tuple((b + turn) % bits for b in range(bits))
+
+
+def place_of(slot, order):
+    top = len(order) - 1
+    return sum(((slot >> bit) & 1) << (top - i) for i, bit in enumerate(order))
+
+
+def slot_at(place, order):
+    top = len(order) - 1
+    return sum(((place >> (top - i)) & 1) << bit for i, bit in enumerate(order))
 
 
 def vmem():
@@ -154,8 +164,12 @@
     return (rows == ids[k : k + 1]).astype(jnp.float32).astype(jnp.bfloat16)
 
 
-def hidden_kernel(first_k, per_k, top, experts, bits, me_ref, got_ref, *refs):
-    weights, (send_ref, keep_ref, own_x, pair_x) = refs[:4], refs[4:]
+def hidden_kernel(
+    first_k, per_k, top, experts, order, sides, has_base, me_ref, got_ref, *refs
+):
+    weights, refs = refs[: 2 * len(sides)], refs[2 * len(sides) :]
+    base_ref, refs = (refs[0], refs[1:]) if has_base else (None, refs)
+    x_refs, outs = refs[-len(sides) :], refs[: -len(sides)]
     tokens = got_ref.shape[0]
     blocks, half, depth = weights[0].shape
     width = depth // experts
@@ -166,31 +180,33 @@
     def _():
         columns, ids, _ = lane_tables(got_ref, 2 * width, top)
         low, high = columns[:width], columns[width:]
-        first = me % 2 == 0
-        for x_ref, part in (
-            (own_x, jnp.where(first, low, high)),
-            (pair_x, jnp.where(first, high, low)),
-        ):
-            wide = spread(part, experts)
+        for side, x_ref in zip(sides, x_refs):
+            wide = spread(jnp.where(me % 2 == side, low, high), experts)
             for k in range(per_k):
                 x_ref[:, :, k * tokens : (k + 1) * tokens] = wide * named(
                     ids, first_k + k, experts
                 )
 
-    lanes = own_x.shape[2]
-    result = jnp.zeros((2 * blocks * half, lanes), jnp.float32)
-    for at, x_ref in ((0, own_x), (2, pair_x)):
-        both = [w_ref[...].reshape(blocks * half, depth) for w_ref in weights[at : at + 2]]
-        result = result + jnp.dot(
+    lanes = x_refs[0].shape[2]
+    rows = blocks * half
+    result = base_ref[...].reshape(2 * rows, lanes) if has_base else None
+    for at, x_ref in enumerate(x_refs):
+        both = [w_ref[...].reshape(rows, depth) for w_ref in weights[2 * at : 2 * at + 2]]
+        term = jnp.dot(
             jnp.concatenate(both, axis=0),
             x_ref[...].reshape(depth, lanes),
             preferred_element_type=jnp.float32,
         )
+        result = term if result is None else result + term
+    if len(outs) == 1:
+        outs[0][...] = result.reshape(outs[0].shape)
+        return
+    send_ref, keep_ref = outs
     count = send_ref.shape[0]
     for b in range(blocks):
         gate = result[b * half : (b + 1) * half]
-        up = result[(blocks + b) * half : (blocks + b + 1) * half]
-        place = flipped((step * blocks + b) ^ (me // 2), bits)
+        up = result[rows + b * half : rows + (b + 1) * half]
+        place = place_of((step * blocks + b) ^ (me // 2), order)
 
         @pl.when(place < count)
         def _():
@@ -227,7 +243,7 @@
     refs[-1][...] = left_terms(chunks, 0, parts, top, experts, width, got_ref, refs[:-1], None)
 
 
-def down_kernel(chunk, first_k, parts, top, experts, base, bits, *refs):
+def down_kernel(chunk, first_k, parts, top, experts, base, orders, *refs):
     me_ref, slot_ref, got_ref, before_ref, down_ref, scale_ref = refs[:6]
     pieces = refs[6:-5]
     send_ref, keep_ref, left_ref, part_ref, expert_ref = refs[-5:]
@@ -249,7 +265,8 @@
     rows = tokens // (2 * count)
     for place in range(2 * count):
         out_ref = keep_ref if place < count else send_ref
-        d = flipped(place, bits) ^ me
+        early, late = (slot_at(place, order) for order in orders)
+        d = jnp.where(pl.program_id(0) < pl.num_programs(0) // 2, early, late) ^ me
         at = pl.multiple_of(d * rows, rows)
         for b in range(base // rows):
             out_ref[place % count, b * rows : (b + 1) * rows, :] = part_ref[
@@ -258,18 +275,19 @@
         out_ref[place % count, base:, :] = scale_ref[expert_ref[d], 0].astype(jnp.float32)
 
 
-def finish_kernel(gate_cols, gate_factor, down_factor, base, extra, *refs):
+def finish_kernel(gate_cols, gate_factor, down_factor, base, extra, count, *refs):
     pieces, (out_ref, scale_ref) = refs[:-2], refs[-2:]
     rows, _ = out_ref.shape
     steps = pieces[0].shape[1] // (base + extra)
+    shared, rest = pieces[:2], pieces[2:]
     for s in range(steps):
         low = s * (base + extra)
-        middle, high = low + base, low + base + extra
-        total = pieces[0][0, low:middle].astype(jnp.float32)
-        largest = pieces[0][0, middle:high].astype(jnp.float32)
-        for piece in pieces[1:]:
-            total = total + piece[0, low:middle].astype(jnp.float32)
-            largest = jnp.maximum(largest, piece[0, middle:high].astype(jnp.float32))
+        terms = [piece[0, low : low + base + extra].astype(jnp.float32) for piece in shared]
+        low = s % (steps // 2) * (base + extra)
+        part = rest[:count] if s < steps // 2 else rest[count:]
+        terms += [piece[0, low : low + base + extra].astype(jnp.float32) for piece in part]
+        total = sum(t[:base] for t in terms)
+        largest = functools.reduce(jnp.maximum, [t[base:] for t in terms])
         for q in range(base // rows):
             at = (s * (base // rows) + q) * LANES
             out_ref[:, at : at + LANES] = total[q * rows : (q + 1) * rows].astype(jnp.bfloat16)
@@ -280,20 +298,18 @@
                 scale_ref[:, at : at + LANES] = largest[q : q + 1] * factor
 
 
-def scatter(send, keep, n, first_bit, stages, merge):
-    whole, pieces, shift = [keep], [keep], first_bit
-    for stage, bits in enumerate(stages):
-        count = 2**bits
-        if stage:
-            size = pieces[0].shape[0] // count
-            send = [merge([p[m * size : (m + 1) * size] for p in pieces]) for m in range(1, count)]
+def scatter(send, pieces, n, first_bit, order, merge):
+    whole = []
+    for bit in order:
+        if send is None:
+            size = pieces[0].shape[0] // 2
+            send = merge([p[size:] for p in pieces])
             pieces = [p[:size] for p in pieces]
-        for m in range(1, count):
-            mask = flipped(m, bits) << shift
-            got = lax.ppermute(send[m - 1], "ep", [(i, i ^ mask) for i in range(n)])
-            whole.append(got)
-            pieces.append(got)
-        shift += bits
+        mask = 1 << (bit + first_bit)
+        got = lax.ppermute(send, "ep", [(i, i ^ mask) for i in range(n)])
+        whole.append(got)
+        pieces = pieces + [got]
+        send = None
     return whole
 
 
@@ -334,7 +350,8 @@
     down_rows, _, _ = down_proj.shape
     all_tokens = n * tok_rows
     depth = gate_rows * experts
-    chunks = CHUNKS if top == sum(CHUNKS) else (top,)
+    plan = CHUNKS if top == sum(size for size, _ in CHUNKS) else ((top, 0),)
+    chunks = tuple(size for size, _ in plan)
     me = lax.axis_index("ep").astype(jnp.int32).reshape(1)
 
     packed = pl.pallas_call(
@@ -375,33 +392,60 @@
 
     blocks = BLOCKS if (n // 2) % BLOCKS == 0 else 2
     all_pieces, first_k = [], 0
-    for per_k in chunks:
+    for c, (per_k, turn) in enumerate(plan):
+        order = bit_order(bits - 1, turn)
         lanes = per_k * all_tokens
+        steps = n // 2 // blocks
         shape = (n // 4, 2 * down_rows, lanes)
-        send, keep = pl.pallas_call(
-            functools.partial(hidden_kernel, first_k, per_k, top, experts, bits - 1),
-            grid=(n // 2 // blocks,),
-            out_shape=(
-                jax.ShapeDtypeStruct(shape, jnp.bfloat16),
-                jax.ShapeDtypeStruct(shape, jnp.float32),
-            ),
-            in_specs=[smem(), vmem()]
-            + [pl.BlockSpec((blocks, down_rows, depth), lambda i: (i, 0, 0))] * 4,
-            out_specs=(pl.BlockSpec(shape, lambda i: (0, 0, 0)),) * 2,
-            scratch_shapes=[pltpu.VMEM((gate_rows, experts, lanes), jnp.bfloat16)] * 2,
-            compiler_params=params(34),
-            cost_estimate=pl.CostEstimate(
-                flops=2 * depth * gate_cols * lanes,
-                bytes_accessed=2 * depth * gate_cols + 3 * gate_cols * lanes // 2,
-                transcendentals=0,
-            ),
-        )(me, got, *own, *pair)
+        pieces_out = (
+            jax.ShapeDtypeStruct(shape, jnp.bfloat16),
+            jax.ShapeDtypeStruct(shape, jnp.float32),
+        )
+        pieces_spec = (pl.BlockSpec(shape, lambda i: (0, 0, 0)),) * 2
+        part = (steps, 2 * blocks * down_rows, lanes)
+        part_spec = pl.BlockSpec((1,) + part[1:], lambda i: (i, 0, 0))
+
+        def hidden(sides, weights, base, out_shape, out_specs):
+            return pl.pallas_call(
+                functools.partial(
+                    hidden_kernel,
+                    first_k,
+                    per_k,
+                    top,
+                    experts,
+                    order,
+                    sides,
+                    len(base) == 1,
+                ),
+                grid=(steps,),
+                out_shape=out_shape,
+                in_specs=[smem(), vmem()]
+                + [pl.BlockSpec((blocks, down_rows, depth), lambda i: (i, 0, 0))]
+                * len(weights)
+                + [part_spec] * len(base),
+                out_specs=out_specs,
+                scratch_shapes=[pltpu.VMEM((gate_rows, experts, lanes), jnp.bfloat16)]
+                * len(sides),
+                compiler_params=params(34),
+                cost_estimate=pl.CostEstimate(
+                    flops=depth * gate_cols * lanes * len(sides),
+                    bytes_accessed=depth * gate_cols * len(sides)
+                    + 3 * gate_cols * lanes // 2,
+                    transcendentals=0,
+                ),
+            )(me, got, *weights, *base)
+
+        if c:
+            send, keep = hidden((0, 1), own + pair, [], pieces_out, pieces_spec)
+        else:
+            base = hidden((0,), own, [], jax.ShapeDtypeStruct(part, jnp.float32), part_spec)
+            send, keep = hidden((1,), pair, [base], pieces_out, pieces_spec)
         first_k += per_k
-        all_pieces += scatter([send], keep, n, 1, HIDDEN_STAGES(bits - 1), add_up)
+        all_pieces += [keep] + scatter(send, [keep], n, 1, order, add_up)
 
     parts = len(all_pieces) // len(chunks)
     scale_cols = gate_cols + model_width
-    steps = OUT_STEPS if model_width % (OUT_STEPS * LANES) == 0 else 1
+    steps = OUT_STEPS if model_width % (OUT_STEPS * LANES) == 0 else 2
     base = tok_rows * model_width // LANES // steps
     extra = -(-scale_cols // (8 * steps * LANES)) * 8
     gate_max = column_max(gate_up, 2)
@@ -424,11 +468,12 @@
         out_specs=vmem(),
         compiler_params=params(16),
     )(got, *early)
+    orders = [(0,) + tuple(b + 1 for b in bit_order(bits - 1, turn)) for turn in range(2)]
     shape = (n // 2, steps * (base + extra), LANES)
     out_block = pl.BlockSpec((n // 2, base + extra, LANES), lambda i: (0, i, 0))
     send, keep = pl.pallas_call(
         functools.partial(
-            down_kernel, chunks[-1], top - chunks[-1], parts, top, experts, base, bits
+            down_kernel, chunks[-1], top - chunks[-1], parts, top, experts, base, orders
         ),
         grid=(steps,),
         out_shape=(jax.ShapeDtypeStruct(shape, jnp.float32),) * 2,
@@ -465,7 +510,11 @@
             jnp.bfloat16
         )
 
-    pieces = scatter([send], keep, n, 0, OUTPUT_STAGES(bits), merge)
+    pieces = [keep] + scatter(send, [keep], n, 0, (0,), merge)
+    middle = steps // 2 * (base + extra)
+    for half, order in enumerate(orders):
+        own = [p[:, half * middle : (half + 1) * middle] for p in pieces[:2]]
+        pieces = pieces + scatter(None, own, n, 0, order[1:], merge)
     return pl.pallas_call(
         functools.partial(
             finish_kernel,
@@ -474,6 +523,7 @@
             math.sqrt(down_rows * n),
             base,
             extra,
+            bits - 1,
         ),
         grid=(1,),
         out_shape=(
@@ -482,16 +532,8 @@
         ),
         in_specs=[first_slot(p) for p in pieces],
         out_specs=(vmem(),) * 2,
-        compiler_params=params(8),
+        compiler_params=params(10),
     )(*pieces)
-
-
-def HIDDEN_STAGES(bits):
-    return [1] * bits
-
-
-def OUTPUT_STAGES(bits):
-    return [1] * bits
 
 
 def shards(tokens, gate_up, down_proj, expert_ids, gate_weights, owner_slot):

time: 121 us -> 123 us (1.017)
  starting transfers between devices: 22.4 us -> 27.5 us
  waiting for transfers between devices: 50.8 us -> 47.6 us
    ppermute x16 -> x19, starting transfers between devices: 14.5 us -> 19.6 us  [scatter(): got = lax.ppermute(send, 'ep', [(i, i ^ mask) for i in range(n)])]
    ppermute x16 -> x19, waiting for transfers between devices: 47.9 us -> 44.7 us  [scatter(): got = lax.ppermute(send, 'ep', [(i, i ^ mask) for i in range(n)])]
    pallas_call x4 -> x5, Pallas kernels: 22.9 us -> 23.7 us  [hidden(): pl.pallas_call(functools.partial(hidden_kernel, first_k, per_k, top, expe...]
    unnamed x13 -> x15, local copies, waits for them, and re-layouts: 6.96 us -> 7.05 us
  transfers between devices with their start and end apart: 19 -> 22, of which waited for: 8 -> 12; matrix products, arithmetic and copies ran while one was open for 0% -> 0% of each run, Pallas kernels for 22% -> 22%
where the time goes in v3:
time: 123 us
  waiting for transfers between devices  47.6 us (39%)
  Pallas kernels  39 us (32%)
  starting transfers between devices  27.5 us (22%)
  local copies, waits for them, and re-layouts  7.06 us (6%)
    ppermute x19, waiting for transfers between devices, scatter(): got = lax.ppermute(send, 'ep', [(i, i ^ mask) for i in range(n)])  44.7 us
    pallas_call x5, Pallas kernels, hidden(): pl.pallas_call(functools.partial(hidden_kernel, first_k, per_k, top, expe...  23.7 us
    ppermute x19, starting transfers between devices, scatter(): got = lax.ppermute(send, 'ep', [(i, i ^ mask) for i in range(n)])  19.6 us
    pallas_call x2, Pallas kernels, row_path(): pl.pallas_call(prep_kernel, grid=(per_half,), out_shape=(half_shape,) * 2...  7.56 us
    all_to_all x1, starting transfers between devices, row_path(): got = lax.all_to_all(packed, 'ep', split_axis=0, concat_axis=0, tiled=True)  7.39 us
    unnamed x15, local copies, waits for them, and re-layouts  7.05 us
    pallas_call x1, Pallas kernels, row_path(): pl.pallas_call(functools.partial(down_kernel, chunks[-1], top - chunks[-1...  3.16 us
    all_to_all x1, waiting for transfers between devices, row_path(): got = lax.all_to_all(packed, 'ep', split_axis=0, concat_axis=0, tiled=True)  2.89 us
  transfers between devices with their start and end apart: 22, of which 12 were waited for; matrix products, arithmetic and copies ran while one was open for 0% of the time, Pallas kernels for 22%

profile of v3, /device:TPU:0, one launch (start us, length us, event | category | flops | bytes accessed | tf_op | source)
XLA Modules:
  0.0 122.9 jit_solution(6425311106108761095)
XLA Ops:
  0.6 3.8 %shard_map.78 = (bf16[8,48,2048]{2,1,0:T(8,128)(2,1)}, bf16[8,48,2048]{2,1,0:T(8,128)(2,1)}) custom-call(s32[1]{0:T(128)} %bitcast.me_ref.refs_0_, bf16[128,16,1536]{2,1,0:T(8,128)(2,1)} %w_ref.2), custom_call_target="tpu_custom_call" | custom-call | flops 3145728 | bytes 6291456 | tf_op jit(solution)/shard_map/pallas_call | solution.py:373
  4.9 3.8 %shard_map.79 = (bf16[8,48,2048]{2,1,0:T(8,128)(2,1)}, bf16[8,48,2048]{2,1,0:T(8,128)(2,1)}) custom-call(s32[1]{0:T(128)} %bitcast.me_ref.refs_0_, bf16[128,16,1536]{2,1,0:T(8,128)(2,1)} %w_ref.2), custom_call_target="tpu_custom_call" | custom-call | flops 3145728 | bytes 6291456 | tf_op jit(solution)/shard_map/pallas_call | solution.py:373
  10.3 7.4 %all-to-all-start = ((bf16[16,16,384]{2,1,0:T(8,128)(2,1)}), bf16[16,16,384]{2,1,0:T(8,128)(2,1)S(1)}, u32[]{:S(2)}, u32[]{:S(2)}) async-start(bf16[16,16,384]{2,1,0:T(8,128)(2,1)} %shard_map.77), calls=%async_computation | async-start | bytes 393216 | tf_op jit(solution)/shard_map/all_to_all | solution.py:364
  17.8 1.9 %copy-done.1 = bf16[48,16,2048]{2,1,0:T(8,128)(2,1)S(1)} copy-done((bf16[48,16,2048]{2,1,0:T(8,128)(2,1)S(1)}, bf16[48,16,2048]{2,1,0:T(8,128)(2,1)}, u32[]{:S(2)}) %copy-start.1) | copy-done | bytes 3145752
  20.1 2.8 %copy-done = bf16[128,16,1536]{2,1,0:T(8,128)(2,1)S(1)} copy-done((bf16[128,16,1536]{2,1,0:T(8,128)(2,1)S(1)}, bf16[128,16,1536]{2,1,0:T(8,128)(2,1)}, u32[]{:S(2)}) %copy-start) | copy-done | bytes 6291480
  23.8 2.9 %all-to-all-done = bf16[16,16,384]{2,1,0:T(8,128)(2,1)S(1)} async-done(((bf16[16,16,384]{2,1,0:T(8,128)(2,1)}), bf16[16,16,384]{2,1,0:T(8,128)(2,1)S(1)}, u32[]{:S(2)}, u32[]{:S(2)}) %all-to-all-start) | async-done | bytes 196640 | tf_op jit(solution)/shard_map/all_to_all | solution.py:364
  28.1 2.5 %shard_map.80.refs_2_ = f32[2,384,512]{2,1,0:T(8,128)S(1)} custom-call(s32[1]{0:T(128)} %bitcast.me_ref.refs_0_, bf16[256,384]{1,0:T(8,128)(2,1)S(1)} %bitcast.10, bf16[8,48,2048]{2,1,0:T(8,128)(2,1)S(1)} %copy-done.3, bf16[8,48,2048]{2,1,0:T(8,128)(2,1)S(1)} %copy-done.4), custom_call_target="tpu_custom_call" | custom-call | flops 1610612736 | bytes 4325376 | tf_op jit(solution)/shard_map/pallas_call | solution.py:409
  30.7 3.9 %shard_map.81 = (bf16[4,96,512]{2,1,0:T(8,128)(2,1)S(1)}, f32[4,96,512]{2,1,0:T(8,128)S(1)}) custom-call(s32[1]{0:T(128)} %bitcast.me_ref.refs_0_, bf16[256,384]{1,0:T(8,128)(2,1)S(1)} %bitcast.11, bf16[8,48,2048]{2,1,0:T(8,128)(2,1)S(1)} %collective-permute-done.refs_0_.refs_2_, bf16[8,48,2048]{2,1,0:T(8,128)(2,1)} %collective-permute-done.1.refs_1_.refs_3_, ...), custom_call_target="tpu_custom_call" | custom-call | flops 1610612736 | bytes 4325376 | tf_op jit(solution)/shard_map/pallas_call | solution.py:409
  34.7 4.1 %shard_map.83 = (bf16[4,96,256]{2,1,0:T(8,128)(2,1)S(1)}, f32[4,96,256]{2,1,0:T(8,128)S(1)}) custom-call(s32[1]{0:T(128)} %bitcast.me_ref.refs_0_, bf16[256,384]{1,0:T(8,128)(2,1)S(1)} %bitcast.12, bf16[8,48,2048]{2,1,0:T(8,128)(2,1)S(1)} %copy-done.3, bf16[8,48,2048]{2,1,0:T(8,128)(2,1)S(1)} %copy-done.5, ...), custom_call_target="tpu_custom_call" | custom-call | flops 1610612736 | bytes 6881280 | tf_op jit(solution)/shard_map/pallas_call | solution.py:409
  39.8 7.4 %shard_map.82 = (bf16[4,96,768]{2,1,0:T(8,128)(2,1)S(1)}, f32[4,96,768]{2,1,0:T(8,128)S(1)}) custom-call(s32[1]{0:T(128)} %bitcast.me_ref.refs_0_, bf16[256,384]{1,0:T(8,128)(2,1)S(1)} %bitcast.13, bf16[8,48,2048]{2,1,0:T(8,128)(2,1)S(1)} %copy-done.3, bf16[8,48,2048]{2,1,0:T(8,128)(2,1)S(1)} %copy-done.5, ...), custom_call_target="tpu_custom_call" | custom-call | flops 4831838208 | bytes 8060928 | tf_op jit(solution)/shard_map/pallas_call | solution.py:409
  48.4 1.9 %collective-permute-start.9 = (bf16[2,96,256]{2,1,0:T(8,128)(2,1)S(1)}, bf16[2,96,256]{2,1,0:T(8,128)(2,1)S(1)}, u32[]{:S(2)}, u32[]{:S(2)}) collective-permute-start(bf16[2,96,256]{2,1,0:T(8,128)(2,1)S(1)} %add_convert_fusion.5), channel_id=1, source_target_pairs={{0,8},{1,9},{2,10},{3,11},{4,12},{5,13},{6,14},{7,15},{8,0},{9,1},... | collective-permute-start | bytes 294920 | tf_op jit(solution)/shard_map/ppermute | solution.py:309
  50.3 5.7 %shard_map.87 = (bf16[4,96,512]{2,1,0:T(8,128)(2,1)S(1)}, f32[4,96,512]{2,1,0:T(8,128)S(1)}) custom-call(s32[1]{0:T(128)} %bitcast.me_ref.refs_0_, bf16[256,384]{1,0:T(8,128)(2,1)S(1)} %bitcast.14, bf16[8,48,2048]{2,1,0:T(8,128)(2,1)S(1)} %copy-done.3, bf16[8,48,2048]{2,1,0:T(8,128)(2,1)S(1)} %copy-done.5, ...), custom_call_target="tpu_custom_call" | custom-call | flops 3221225472 | bytes 7471104 | tf_op jit(solution)/shard_map/pallas_call | solution.py:409
  59.2 11.8 %collective-permute-done.11.refs_7_ = bf16[4,96,512]{2,1,0:T(8,128)(2,1)S(1)} collective-permute-done((bf16[4,96,512]{2,1,0:T(8,128)(2,1)S(1)}, bf16[4,96,512]{2,1,0:T(8,128)(2,1)S(1)}, u32[]{:S(2)}, u32[]{:S(2)}) %collective-permute-start.11) | collective-permute-done | bytes 393248 | tf_op jit(solution)/shard_map/ppermute | solution.py:309
  73.3 2.4 %collective-permute-start.4 = (bf16[1,96,512]{2,1,0:T(8,128)(2,1)S(1)}, bf16[1,96,512]{2,1,0:T(8,128)(2,1)S(1)}, u32[]{:S(2)}, u32[]{:S(2)}) collective-permute-start(bf16[1,96,512]{2,1,0:T(8,128)(2,1)S(1)} %add_convert_fusion.6), channel_id=1, source_target_pairs={{0,8},{1,9},{2,10},{3,11},{4,12},{5,13},{6,14},{7,15},{8,0},{9,1},... | collective-permute-start | bytes 294920 | tf_op jit(solution)/shard_map/ppermute | solution.py:309
  75.8 6.2 %collective-permute-done.12.refs_8_ = bf16[2,96,512]{2,1,0:T(8,128)(2,1)S(1)} collective-permute-done((bf16[2,96,512]{2,1,0:T(8,128)(2,1)S(1)}, bf16[2,96,512]{2,1,0:T(8,128)(2,1)S(1)}, u32[]{:S(2)}, u32[]{:S(2)}) %collective-permute-start.12) | collective-permute-done | bytes 196640 | tf_op jit(solution)/shard_map/ppermute | solution.py:309
  82.5 3.1 %collective-permute-done.6.refs_6_ = bf16[2,96,768]{2,1,0:T(8,128)(2,1)S(1)} collective-permute-done((bf16[2,96,768]{2,1,0:T(8,128)(2,1)S(1)}, bf16[2,96,768]{2,1,0:T(8,128)(2,1)S(1)}, u32[]{:S(2)}, u32[]{:S(2)}) %collective-permute-start.6) | collective-permute-done | bytes 294944 | tf_op jit(solution)/shard_map/ppermute | solution.py:309
  87.1 8.7 %collective-permute-done.7.refs_7_ = bf16[1,96,768]{2,1,0:T(8,128)(2,1)S(1)} collective-permute-done((bf16[1,96,768]{2,1,0:T(8,128)(2,1)S(1)}, bf16[1,96,768]{2,1,0:T(8,128)(2,1)S(1)}, u32[]{:S(2)}, u32[]{:S(2)}) %collective-permute-start.7) | collective-permute-done | bytes 147488 | tf_op jit(solution)/shard_map/ppermute | solution.py:309
  97.7 3.2 %shard_map.88 = (f32[8,288,128]{2,1,0:T(8,128)S(1)}, f32[8,288,128]{2,1,0:T(8,128)S(1)}) custom-call(s32[1]{0:T(128)} %bitcast.me_ref.refs_0_, s32[16]{0:T(128)S(1)} %copy-done.6, bf16[256,384]{1,0:T(8,128)(2,1)S(1)} %bitcast.16, bf16[48,16,256]{2,1,0:T(8,128)(2,1)S(1)} %shard_map.84.refs_3_, bf16[768,2048]{1,0:T(8,128)(2,1)S(1)} %bitcast.9, ...), custom_call_target="tpu_custom_call" | custom-call | tf_op jit(solution)/shard_map/pallas_call | solution.py:474
  101.0 2.8 %collective-permute-done.14.refs_1_ = f32[8,288,128]{2,1,0:T(8,128)S(1)} collective-permute-done((f32[8,288,128]{2,1,0:T(8,128)S(1)}, f32[8,288,128]{2,1,0:T(8,128)S(1)}, u32[]{:S(2)}, u32[]{:S(2)}) %collective-permute-start.14) | collective-permute-done | bytes 1179680 | tf_op jit(solution)/shard_map/ppermute | solution.py:309
  104.7 5.3 %collective-permute-done.15.refs_2_ = bf16[4,144,128]{2,1,0:T(8,128)(2,1)S(1)} collective-permute-done((bf16[4,144,128]{2,1,0:T(8,128)(2,1)S(1)}, bf16[4,144,128]{2,1,0:T(8,128)(2,1)S(1)}, u32[]{:S(2)}, u32[]{:S(2)}) %collective-permute-start.15) | collective-permute-done | bytes 147488 | tf_op jit(solution)/shard_map/ppermute | solution.py:309
  110.8 2.0 %collective-permute-start.19 = (bf16[2,144,128]{2,1,0:T(8,128)(2,1)S(1)}, bf16[2,144,128]{2,1,0:T(8,128)(2,1)S(1)}, u32[]{:S(2)}, u32[]{:S(2)}) collective-permute-start(bf16[2,144,128]{2,1,0:T(8,128)(2,1)S(1)} %get-tuple-element.32), channel_id=1, source_target_pairs={{0,8},{1,9},{2,10},{3,11},{4,12},{5,13},{6,14},{7,15},{8,0},{9,1},... | collective-permute-start | bytes 221192 | tf_op jit(solution)/shard_map/ppermute | solution.py:309
  112.8 2.1 %collective-permute-done.16.refs_3_ = bf16[2,144,128]{2,1,0:T(8,128)(2,1)S(1)} collective-permute-done((bf16[2,144,128]{2,1,0:T(8,128)(2,1)S(1)}, bf16[2,144,128]{2,1,0:T(8,128)(2,1)S(1)}, u32[]{:S(2)}, u32[]{:S(2)}) %collective-permute-start.16) | collective-permute-done | bytes 73760 | tf_op jit(solution)/shard_map/ppermute | solution.py:309
  116.4 1.8 %collective-permute-start.17 = (bf16[1,144,128]{2,1,0:T(8,128)(2,1)S(1)}, bf16[1,144,128]{2,1,0:T(8,128)(2,1)S(1)}, u32[]{:S(2)}, u32[]{:S(2)}) collective-permute-start(bf16[1,144,128]{2,1,0:T(8,128)(2,1)S(1)} %get-tuple-element.31), channel_id=1, source_target_pairs={{0,8},{1,9},{2,10},{3,11},{4,12},{5,13},{6,14},{7,15},{8,0},{9,1},... | collective-permute-start | bytes 110600 | tf_op jit(solution)/shard_map/ppermute | solution.py:309
  119.3 2.1 %collective-permute-done.17.refs_4_ = bf16[1,144,128]{2,1,0:T(8,128)(2,1)S(1)} collective-permute-done((bf16[1,144,128]{2,1,0:T(8,128)(2,1)S(1)}, bf16[1,144,128]{2,1,0:T(8,128)(2,1)S(1)}, u32[]{:S(2)}, u32[]{:S(2)}) %collective-permute-start.17) | collective-permute-done | bytes 36896 | tf_op jit(solution)/shard_map/ppermute | solution.py:309
  (64 shorter events, 22.4 us)
Async XLA Ops:
  4.4 26.2 %collective-permute-start = (bf16[8,48,2048]{2,1,0:T(8,128)(2,1)}, bf16[8,48,2048]{2,1,0:T(8,128)(2,1)S(1)}, u32[]{:S(2)}, u32[]{:S(2)}) collective-permute-start(bf16[8,48,2048]{2,1,0:T(8,128)(2,1)} %get-tuple-element.16), channel_id=1, source_target_pairs={{0,1},{1,0},{2,3},{3,2},{4,5},{5,4},{6,7},{7,6},{8,9},{9,8},{10,11... | collective-permute-start | bytes 4718600 | tf_op jit(solution)/shard_map/ppermute | solution.py:390
  8.7 22.0 %collective-permute-start.1 = (bf16[8,48,2048]{2,1,0:T(8,128)(2,1)}, bf16[8,48,2048]{2,1,0:T(8,128)(2,1)}, u32[]{:S(2)}, u32[]{:S(2)}) collective-permute-start(bf16[8,48,2048]{2,1,0:T(8,128)(2,1)} %get-tuple-element.17), channel_id=1, source_target_pairs={{0,1},{1,0},{2,3},{3,2},{4,5},{5,4},{6,7},{7,6},{8,9},{9,8},{10,11... | collective-permute-start | bytes 4718600 | tf_op jit(solution)/shard_map/ppermute | solution.py:390
  10.3 16.4 %all-to-all-start = ((bf16[16,16,384]{2,1,0:T(8,128)(2,1)}), bf16[16,16,384]{2,1,0:T(8,128)(2,1)S(1)}, u32[]{:S(2)}, u32[]{:S(2)}) async-start(bf16[16,16,384]{2,1,0:T(8,128)(2,1)} %shard_map.77), calls=%async_computation | async-start | bytes 393216 | tf_op jit(solution)/shard_map/all_to_all | solution.py:364
  30.6 4.0 %copy-start.5 = (bf16[8,48,2048]{2,1,0:T(8,128)(2,1)S(1)}, bf16[8,48,2048]{2,1,0:T(8,128)(2,1)}, u32[]{:S(2)}) copy-start(bf16[8,48,2048]{2,1,0:T(8,128)(2,1)} %get-tuple-element.19.refs_1_) | copy-start | bytes 4718596
  34.6 23.6 %collective-permute-start.2 = (bf16[4,96,512]{2,1,0:T(8,128)(2,1)S(1)}, bf16[4,96,512]{2,1,0:T(8,128)(2,1)S(1)}, u32[]{:S(2)}, u32[]{:S(2)}) collective-permute-start(bf16[4,96,512]{2,1,0:T(8,128)(2,1)S(1)} %get-tuple-element.21), channel_id=1, source_target_pairs={{0,2},{1,3},{2,0},{3,1},{4,6},{5,7},{6,4},{7,5},{8,10},{9,11},{10,... | collective-permute-start | bytes 1179656 | tf_op jit(solution)/shard_map/ppermute | solution.py:309
  38.8 9.6 %collective-permute-start.8 = (bf16[4,96,256]{2,1,0:T(8,128)(2,1)S(1)}, bf16[4,96,256]{2,1,0:T(8,128)(2,1)S(1)}, u32[]{:S(2)}, u32[]{:S(2)}) collective-permute-start(bf16[4,96,256]{2,1,0:T(8,128)(2,1)S(1)} %get-tuple-element.25), channel_id=1, source_target_pairs={{0,4},{1,5},{2,6},{3,7},{4,0},{5,1},{6,2},{7,3},{8,12},{9,13},{10,... | collective-permute-start | bytes 589832 | tf_op jit(solution)/shard_map/ppermute | solution.py:309
  47.2 25.1 %collective-permute-start.5 = (bf16[4,96,768]{2,1,0:T(8,128)(2,1)S(1)}, bf16[4,96,768]{2,1,0:T(8,128)(2,1)S(1)}, u32[]{:S(2)}, u32[]{:S(2)}) collective-permute-start(bf16[4,96,768]{2,1,0:T(8,128)(2,1)S(1)} %get-tuple-element.23), channel_id=1, source_target_pairs={{0,2},{1,3},{2,0},{3,1},{4,6},{5,7},{6,4},{7,5},{8,10},{9,11},{10,... | collective-permute-start | bytes 1769480 | tf_op jit(solution)/shard_map/ppermute | solution.py:309
  48.4 9.2 %collective-permute-start.9 = (bf16[2,96,256]{2,1,0:T(8,128)(2,1)S(1)}, bf16[2,96,256]{2,1,0:T(8,128)(2,1)S(1)}, u32[]{:S(2)}, u32[]{:S(2)}) collective-permute-start(bf16[2,96,256]{2,1,0:T(8,128)(2,1)S(1)} %add_convert_fusion.5), channel_id=1, source_target_pairs={{0,8},{1,9},{2,10},{3,11},{4,12},{5,13},{6,14},{7,15},{8,0},{9,1},... | collective-permute-start | bytes 294920 | tf_op jit(solution)/shard_map/ppermute | solution.py:309
  56.0 15.0 %collective-permute-start.11 = (bf16[4,96,512]{2,1,0:T(8,128)(2,1)S(1)}, bf16[4,96,512]{2,1,0:T(8,128)(2,1)S(1)}, u32[]{:S(2)}, u32[]{:S(2)}) collective-permute-start(bf16[4,96,512]{2,1,0:T(8,128)(2,1)S(1)} %get-tuple-element.27), channel_id=1, source_target_pairs={{0,2},{1,3},{2,0},{3,1},{4,6},{5,7},{6,4},{7,5},{8,10},{9,11},{10,... | collective-permute-start | bytes 1179656 | tf_op jit(solution)/shard_map/ppermute | solution.py:309
  57.6 29.5 %collective-permute-start.10 = (bf16[1,96,256]{2,1,0:T(8,128)(2,1)S(1)}, bf16[1,96,256]{2,1,0:T(8,128)(2,1)S(1)}, u32[]{:S(2)}, u32[]{:S(2)}) collective-permute-start(bf16[1,96,256]{2,1,0:T(8,128)(2,1)S(1)} %add_convert_fusion.7), channel_id=1, source_target_pairs={{0,2},{1,3},{2,0},{3,1},{4,6},{5,7},{6,4},{7,5},{8,10},{9,11},{10,... | collective-permute-start | bytes 147464 | tf_op jit(solution)/shard_map/ppermute | solution.py:309
  58.3 15.0 %collective-permute-start.3 = (bf16[2,96,512]{2,1,0:T(8,128)(2,1)S(1)}, bf16[2,96,512]{2,1,0:T(8,128)(2,1)S(1)}, u32[]{:S(2)}, u32[]{:S(2)}) collective-permute-start(bf16[2,96,512]{2,1,0:T(8,128)(2,1)S(1)} %add_convert_fusion.2), channel_id=1, source_target_pairs={{0,4},{1,5},{2,6},{3,7},{4,0},{5,1},{6,2},{7,3},{8,12},{9,13},{10,... | collective-permute-start | bytes 589832 | tf_op jit(solution)/shard_map/ppermute | solution.py:309
  71.1 10.9 %collective-permute-start.12 = (bf16[2,96,512]{2,1,0:T(8,128)(2,1)S(1)}, bf16[2,96,512]{2,1,0:T(8,128)(2,1)S(1)}, u32[]{:S(2)}, u32[]{:S(2)}) collective-permute-start(bf16[2,96,512]{2,1,0:T(8,128)(2,1)S(1)} %add_convert_fusion.1), channel_id=1, source_target_pairs={{0,4},{1,5},{2,6},{3,7},{4,0},{5,1},{6,2},{7,3},{8,12},{9,13},{10,... | collective-permute-start | bytes 589832 | tf_op jit(solution)/shard_map/ppermute | solution.py:309
  72.4 13.2 %collective-permute-start.6 = (bf16[2,96,768]{2,1,0:T(8,128)(2,1)S(1)}, bf16[2,96,768]{2,1,0:T(8,128)(2,1)S(1)}, u32[]{:S(2)}, u32[]{:S(2)}) collective-permute-start(bf16[2,96,768]{2,1,0:T(8,128)(2,1)S(1)} %add_convert_fusion), channel_id=1, source_target_pairs={{0,4},{1,5},{2,6},{3,7},{4,0},{5,1},{6,2},{7,3},{8,12},{9,13},{10,... | collective-permute-start | bytes 884744 | tf_op jit(solution)/shard_map/ppermute | solution.py:309
  73.3 13.8 %collective-permute-start.4 = (bf16[1,96,512]{2,1,0:T(8,128)(2,1)S(1)}, bf16[1,96,512]{2,1,0:T(8,128)(2,1)S(1)}, u32[]{:S(2)}, u32[]{:S(2)}) collective-permute-start(bf16[1,96,512]{2,1,0:T(8,128)(2,1)S(1)} %add_convert_fusion.6), channel_id=1, source_target_pairs={{0,8},{1,9},{2,10},{3,11},{4,12},{5,13},{6,14},{7,15},{8,0},{9,1},... | collective-permute-start | bytes 294920 | tf_op jit(solution)/shard_map/ppermute | solution.py:309
  82.0 14.8 %collective-permute-start.13 = (bf16[1,96,512]{2,1,0:T(8,128)(2,1)S(1)}, bf16[1,96,512]{2,1,0:T(8,128)(2,1)S(1)}, u32[]{:S(2)}, u32[]{:S(2)}) collective-permute-start(bf16[1,96,512]{2,1,0:T(8,128)(2,1)S(1)} %add_convert_fusion.4), channel_id=1, source_target_pairs={{0,8},{1,9},{2,10},{3,11},{4,12},{5,13},{6,14},{7,15},{8,0},{9,1},... | collective-permute-start | bytes 294920 | tf_op jit(solution)/shard_map/ppermute | solution.py:309
  85.7 10.2 %collective-permute-start.7 = (bf16[1,96,768]{2,1,0:T(8,128)(2,1)S(1)}, bf16[1,96,768]{2,1,0:T(8,128)(2,1)S(1)}, u32[]{:S(2)}, u32[]{:S(2)}) collective-permute-start(bf16[1,96,768]{2,1,0:T(8,128)(2,1)S(1)} %add_convert_fusion.3), channel_id=1, source_target_pairs={{0,8},{1,9},{2,10},{3,11},{4,12},{5,13},{6,14},{7,15},{8,0},{9,1},... | collective-permute-start | bytes 442376 | tf_op jit(solution)/shard_map/ppermute | solution.py:309
  87.1 9.7 %copy-start.6 = (s32[16]{0:T(128)S(1)}, s32[16]{0:T(128)}, u32[]{:S(2)}) copy-start(s32[16]{0:T(128)} %refs_1_.1) | copy-start | bytes 196
  100.9 2.9 %collective-permute-start.14 = (f32[8,288,128]{2,1,0:T(8,128)S(1)}, f32[8,288,128]{2,1,0:T(8,128)S(1)}, u32[]{:S(2)}, u32[]{:S(2)}) collective-permute-start(f32[8,288,128]{2,1,0:T(8,128)S(1)} %get-tuple-element.29), channel_id=1, source_target_pairs={{0,1},{1,0},{2,3},{3,2},{4,5},{5,4},{6,7},{7,6},{8,9},{9,8},{10,11... | collective-permute-start | bytes 3538952 | tf_op jit(solution)/shard_map/ppermute | solution.py:309
  104.1 6.0 %collective-permute-start.15 = (bf16[4,144,128]{2,1,0:T(8,128)(2,1)S(1)}, bf16[4,144,128]{2,1,0:T(8,128)(2,1)S(1)}, u32[]{:S(2)}, u32[]{:S(2)}) collective-permute-start(bf16[4,144,128]{2,1,0:T(8,128)(2,1)S(1)} %get-tuple-element.35), channel_id=1, source_target_pairs={{0,2},{1,3},{2,0},{3,1},{4,6},{5,7},{6,4},{7,5},{8,10},{9,11},{10,... | collective-permute-start | bytes 442376 | tf_op jit(solution)/shard_map/ppermute | solution.py:309
  104.7 5.6 %collective-permute-start.18 = (bf16[4,144,128]{2,1,0:T(8,128)(2,1)S(1)}, bf16[4,144,128]{2,1,0:T(8,128)(2,1)S(1)}, u32[]{:S(2)}, u32[]{:S(2)}) collective-permute-start(bf16[4,144,128]{2,1,0:T(8,128)(2,1)S(1)} %get-tuple-element.34), channel_id=1, source_target_pairs={{0,4},{1,5},{2,6},{3,7},{4,0},{5,1},{6,2},{7,3},{8,12},{9,13},{10,... | collective-permute-start | bytes 442376 | tf_op jit(solution)/shard_map/ppermute | solution.py:309
  110.5 4.4 %collective-permute-start.16 = (bf16[2,144,128]{2,1,0:T(8,128)(2,1)S(1)}, bf16[2,144,128]{2,1,0:T(8,128)(2,1)S(1)}, u32[]{:S(2)}, u32[]{:S(2)}) collective-permute-start(bf16[2,144,128]{2,1,0:T(8,128)(2,1)S(1)} %get-tuple-element.33), channel_id=1, source_target_pairs={{0,4},{1,5},{2,6},{3,7},{4,0},{5,1},{6,2},{7,3},{8,12},{9,13},{10,... | collective-permute-start | bytes 221192 | tf_op jit(solution)/shard_map/ppermute | solution.py:309
  110.8 5.5 %collective-permute-start.19 = (bf16[2,144,128]{2,1,0:T(8,128)(2,1)S(1)}, bf16[2,144,128]{2,1,0:T(8,128)(2,1)S(1)}, u32[]{:S(2)}, u32[]{:S(2)}) collective-permute-start(bf16[2,144,128]{2,1,0:T(8,128)(2,1)S(1)} %get-tuple-element.32), channel_id=1, source_target_pairs={{0,8},{1,9},{2,10},{3,11},{4,12},{5,13},{6,14},{7,15},{8,0},{9,1},... | collective-permute-start | bytes 221192 | tf_op jit(solution)/shard_map/ppermute | solution.py:309
  116.4 4.9 %collective-permute-start.17 = (bf16[1,144,128]{2,1,0:T(8,128)(2,1)S(1)}, bf16[1,144,128]{2,1,0:T(8,128)(2,1)S(1)}, u32[]{:S(2)}, u32[]{:S(2)}) collective-permute-start(bf16[1,144,128]{2,1,0:T(8,128)(2,1)S(1)} %get-tuple-element.31), channel_id=1, source_target_pairs={{0,8},{1,9},{2,10},{3,11},{4,12},{5,13},{6,14},{7,15},{8,0},{9,1},... | collective-permute-start | bytes 110600 | tf_op jit(solution)/shard_map/ppermute | solution.py:309
  118.3 4.0 %collective-permute-start.20 = (bf16[1,144,128]{2,1,0:T(8,128)(2,1)S(1)}, bf16[1,144,128]{2,1,0:T(8,128)(2,1)S(1)}, u32[]{:S(2)}, u32[]{:S(2)}) collective-permute-start(bf16[1,144,128]{2,1,0:T(8,128)(2,1)S(1)} %get-tuple-element.30), channel_id=1, source_target_pairs={{0,2},{1,3},{2,0},{3,1},{4,6},{5,7},{6,4},{7,5},{8,10},{9,11},{10,... | collective-permute-start | bytes 110600 | tf_op jit(solution)/shard_map/ppermute | solution.py:309
  (5 other events, 11.8 us)

commit v4 on v3

--- a/solution.py
+++ b/solution.py
@@ -11,9 +11,11 @@
 
 LANES = 128
 CHUNKS = ((2, 0), (3, 0), (1, 1), (2, 0))
-BLOCKS = 4
-OUT_STEPS = 4
+GROUPS = (1, 2, 1)
+BLOCKS = 8
+OUT_STEPS = 2
 PREP_MIB = 58
+HID_MIB = 34
 
 
 def expert_block(arrived, held_up, held_down):
@@ -165,7 +167,7 @@
 
 
 def hidden_kernel(
-    first_k, per_k, top, experts, order, sides, has_base, me_ref, got_ref, *refs
+    first_k, parts, top, experts, sides, has_base, me_ref, got_ref, *refs
 ):
     weights, refs = refs[: 2 * len(sides)], refs[2 * len(sides) :]
     base_ref, refs = (refs[0], refs[1:]) if has_base else (None, refs)
@@ -182,7 +184,7 @@
         low, high = columns[:width], columns[width:]
         for side, x_ref in zip(sides, x_refs):
             wide = spread(jnp.where(me % 2 == side, low, high), experts)
-            for k in range(per_k):
+            for k in range(x_ref.shape[2] // tokens):
                 x_ref[:, :, k * tokens : (k + 1) * tokens] = wide * named(
                     ids, first_k + k, experts
                 )
@@ -201,22 +203,26 @@
     if len(outs) == 1:
         outs[0][...] = result.reshape(outs[0].shape)
         return
-    send_ref, keep_ref = outs
-    count = send_ref.shape[0]
-    for b in range(blocks):
-        gate = result[b * half : (b + 1) * half]
-        up = result[rows + b * half : rows + (b + 1) * half]
-        place = place_of((step * blocks + b) ^ (me // 2), order)
-
-        @pl.when(place < count)
-        def _():
-            keep_ref[place, :half] = gate
-            keep_ref[place, half:] = up
-
-        @pl.when(place >= count)
-        def _():
-            send_ref[place - count, :half] = gate.astype(jnp.bfloat16)
-            send_ref[place - count, half:] = up.astype(jnp.bfloat16)
+    low = 0
+    for at, (per_k, order) in enumerate(parts):
+        send_ref, keep_ref = outs[2 * at : 2 * at + 2]
+        piece = result[:, low * tokens : (low + per_k) * tokens]
+        low += per_k
+        count = send_ref.shape[0]
+        for b in range(blocks):
+            gate = piece[b * half : (b + 1) * half]
+            up = piece[rows + b * half : rows + (b + 1) * half]
+            place = place_of((step * blocks + b) ^ (me // 2), order)
+
+            @pl.when(place < count)
+            def _():
+                keep_ref[place, :half] = gate
+                keep_ref[place, half:] = up
+
+            @pl.when(place >= count)
+            def _():
+                send_ref[place - count, :half] = gate.astype(jnp.bfloat16)
+                send_ref[place - count, half:] = up.astype(jnp.bfloat16)
 
 
 def left_terms(chunks, first_k, parts, top, experts, width, got_ref, pieces, left):
@@ -391,31 +397,26 @@
         own.append(keep)
 
     blocks = BLOCKS if (n // 2) % BLOCKS == 0 else 2
-    all_pieces, first_k = [], 0
-    for c, (per_k, turn) in enumerate(plan):
-        order = bit_order(bits - 1, turn)
-        lanes = per_k * all_tokens
-        steps = n // 2 // blocks
-        shape = (n // 4, 2 * down_rows, lanes)
-        pieces_out = (
-            jax.ShapeDtypeStruct(shape, jnp.bfloat16),
-            jax.ShapeDtypeStruct(shape, jnp.float32),
-        )
-        pieces_spec = (pl.BlockSpec(shape, lambda i: (0, 0, 0)),) * 2
+    steps = n // 2 // blocks
+    groups = GROUPS if len(plan) == sum(GROUPS) else (1,) * len(plan)
+    all_pieces, c = [], 0
+    for group in groups:
+        first_k = sum(chunks[:c])
+        parts = [(size, bit_order(bits - 1, turn)) for size, turn in plan[c : c + group]]
+        lanes = sum(size for size, _ in parts) * all_tokens
+        out_shape = []
+        for size, _ in parts:
+            shape = (n // 4, 2 * down_rows, size * all_tokens)
+            out_shape.append(jax.ShapeDtypeStruct(shape, jnp.bfloat16))
+            out_shape.append(jax.ShapeDtypeStruct(shape, jnp.float32))
+        out_specs = [pl.BlockSpec(o.shape, lambda i: (0, 0, 0)) for o in out_shape]
         part = (steps, 2 * blocks * down_rows, lanes)
         part_spec = pl.BlockSpec((1,) + part[1:], lambda i: (i, 0, 0))
 
         def hidden(sides, weights, base, out_shape, out_specs):
             return pl.pallas_call(
                 functools.partial(
-                    hidden_kernel,
-                    first_k,
-                    per_k,
-                    top,
-                    experts,
-                    order,
-                    sides,
-                    len(base) == 1,
+                    hidden_kernel, first_k, parts, top, experts, sides, len(base) == 1
                 ),
                 grid=(steps,),
                 out_shape=out_shape,
@@ -426,7 +427,7 @@
                 out_specs=out_specs,
                 scratch_shapes=[pltpu.VMEM((gate_rows, experts, lanes), jnp.bfloat16)]
                 * len(sides),
-                compiler_params=params(34),
+                compiler_params=params(HID_MIB),
                 cost_estimate=pl.CostEstimate(
                     flops=depth * gate_cols * lanes * len(sides),
                     bytes_accessed=depth * gate_cols * len(sides)
@@ -436,12 +437,14 @@
             )(me, got, *weights, *base)
 
         if c:
-            send, keep = hidden((0, 1), own + pair, [], pieces_out, pieces_spec)
+            made = hidden((0, 1), own + pair, [], out_shape, out_specs)
         else:
             base = hidden((0,), own, [], jax.ShapeDtypeStruct(part, jnp.float32), part_spec)
-            send, keep = hidden((1,), pair, [base], pieces_out, pieces_spec)
-        first_k += per_k
-        all_pieces += [keep] + scatter(send, [keep], n, 1, order, add_up)
+            made = hidden((1,), pair, [base], out_shape, out_specs)
+        for at, (_, order) in enumerate(parts):
+            send, keep = made[2 * at : 2 * at + 2]
+            all_pieces += [keep] + scatter(send, [keep], n, 1, order, add_up)
+            c += 1
 
     parts = len(all_pieces) // len(chunks)
     scale_cols = gate_cols + model_width

time: 123 us -> 128 us (1.041)
  waiting for transfers between devices: 47.6 us -> 56.6 us
  Pallas kernels: 39 us -> 35.6 us
    ppermute x19, waiting for transfers between devices: 44.7 us -> 53.7 us  [scatter(): got = lax.ppermute(send, 'ep', [(i, i ^ mask) for i in range(n)])]
    pallas_call x5 -> x4, Pallas kernels: 23.7 us -> 20.7 us  [hidden(): pl.pallas_call(functools.partial(hidden_kernel, first_k, parts, top, expe...]
  transfers between devices with their start and end apart: 22 -> 22, of which waited for: 12 -> 13; matrix products, arithmetic and copies ran while one was open for 0% -> 0% of each run, Pallas kernels for 22% -> 15%
where the time goes in v4:
time: 128 us
  waiting for transfers between devices  56.6 us (44%)
  Pallas kernels  35.6 us (28%)
  starting transfers between devices  26.7 us (21%)
  local copies, waits for them, and re-layouts  7.05 us (6%)
    ppermute x19, waiting for transfers between devices, scatter(): got = lax.ppermute(send, 'ep', [(i, i ^ mask) for i in range(n)])  53.7 us
    pallas_call x4, Pallas kernels, hidden(): pl.pallas_call(functools.partial(hidden_kernel, first_k, parts, top, expe...  20.7 us
    ppermute x19, starting transfers between devices, scatter(): got = lax.ppermute(send, 'ep', [(i, i ^ mask) for i in range(n)])  18.8 us
    pallas_call x2, Pallas kernels, row_path(): pl.pallas_call(prep_kernel, grid=(per_half,), out_shape=(half_shape,) * 2...  7.62 us
    all_to_all x1, starting transfers between devices, row_path(): got = lax.all_to_all(packed, 'ep', split_axis=0, concat_axis=0, tiled=True)  7.39 us
    unnamed x15, local copies, waits for them, and re-layouts  7.04 us
    all_to_all x1, waiting for transfers between devices, row_path(): got = lax.all_to_all(packed, 'ep', split_axis=0, concat_axis=0, tiled=True)  2.89 us
    pallas_call x1, Pallas kernels, row_path(): pl.pallas_call(functools.partial(down_kernel, chunks[-1], top - chunks[-1...  2.66 us
  transfers between devices with their start and end apart: 22, of which 13 were waited for; matrix products, arithmetic and copies ran while one was open for 0% of the time, Pallas kernels for 15%

profile of v4, /device:TPU:0, one launch (start us, length us, event | category | flops | bytes accessed | tf_op | source)
XLA Modules:
  0.0 127.5 jit_solution(2984231405463819303)
XLA Ops:
  0.6 3.8 %shard_map.78 = (bf16[8,48,2048]{2,1,0:T(8,128)(2,1)}, bf16[8,48,2048]{2,1,0:T(8,128)(2,1)}) custom-call(s32[1]{0:T(128)} %bitcast.me_ref.refs_0_, bf16[128,16,1536]{2,1,0:T(8,128)(2,1)} %w_ref.2), custom_call_target="tpu_custom_call" | custom-call | flops 3145728 | bytes 6291456 | tf_op jit(solution)/shard_map/pallas_call | solution.py:379
  4.9 3.8 %shard_map.79 = (bf16[8,48,2048]{2,1,0:T(8,128)(2,1)}, bf16[8,48,2048]{2,1,0:T(8,128)(2,1)}) custom-call(s32[1]{0:T(128)} %bitcast.me_ref.refs_0_, bf16[128,16,1536]{2,1,0:T(8,128)(2,1)} %w_ref.2), custom_call_target="tpu_custom_call" | custom-call | flops 3145728 | bytes 6291456 | tf_op jit(solution)/shard_map/pallas_call | solution.py:379
  10.4 7.4 %all-to-all-start = ((bf16[16,16,384]{2,1,0:T(8,128)(2,1)}), bf16[16,16,384]{2,1,0:T(8,128)(2,1)S(1)}, u32[]{:S(2)}, u32[]{:S(2)}) async-start(bf16[16,16,384]{2,1,0:T(8,128)(2,1)} %shard_map.77), calls=%async_computation | async-start | bytes 393216 | tf_op jit(solution)/shard_map/all_to_all | solution.py:370
  17.8 1.9 %copy-done.1 = bf16[48,16,2048]{2,1,0:T(8,128)(2,1)S(1)} copy-done((bf16[48,16,2048]{2,1,0:T(8,128)(2,1)S(1)}, bf16[48,16,2048]{2,1,0:T(8,128)(2,1)}, u32[]{:S(2)}) %copy-start.1) | copy-done | bytes 3145752
  20.2 2.8 %copy-done = bf16[128,16,1536]{2,1,0:T(8,128)(2,1)S(1)} copy-done((bf16[128,16,1536]{2,1,0:T(8,128)(2,1)S(1)}, bf16[128,16,1536]{2,1,0:T(8,128)(2,1)}, u32[]{:S(2)}) %copy-start) | copy-done | bytes 6291480
  23.9 2.9 %all-to-all-done = bf16[16,16,384]{2,1,0:T(8,128)(2,1)S(1)} async-done(((bf16[16,16,384]{2,1,0:T(8,128)(2,1)}), bf16[16,16,384]{2,1,0:T(8,128)(2,1)S(1)}, u32[]{:S(2)}, u32[]{:S(2)}) %all-to-all-start) | async-done | bytes 196640 | tf_op jit(solution)/shard_map/all_to_all | solution.py:370
  28.2 9.0 %shard_map.82 = (bf16[4,96,768]{2,1,0:T(8,128)(2,1)S(1)}, f32[4,96,768]{2,1,0:T(8,128)S(1)}, bf16[4,96,256]{2,1,0:T(8,128)(2,1)S(1)}, f32[4,96,256]{2,1,0:T(8,128)S(1)}) custom-call(s32[1]{0:T(128)} %bitcast.me_ref.refs_0_, bf16[256,384]{1,0:T(8,128)(2,1)S(1)} %bitcast.10, bf16[8,48,2048]{2,1,0:T(8,128)(2,1)S(1)} %copy-done.4, ...), custom_call_target="tpu_custom_call" | custom-call | flops 6442450944 | bytes 8650752 | tf_op jit(solution)/shard_map/pallas_call | solution.py:417
  37.3 2.1 %shard_map.80.refs_2_ = f32[1,768,512]{2,1,0:T(8,128)S(1)} custom-call(s32[1]{0:T(128)} %bitcast.me_ref.refs_0_, bf16[256,384]{1,0:T(8,128)(2,1)S(1)} %bitcast.11, bf16[8,48,2048]{2,1,0:T(8,128)(2,1)S(1)} %copy-done.4, bf16[8,48,2048]{2,1,0:T(8,128)(2,1)S(1)} %copy-done.5), custom_call_target="tpu_custom_call" | custom-call | flops 1610612736 | bytes 4325376 | tf_op jit(solution)/shard_map/pallas_call | solution.py:417
  39.4 4.0 %shard_map.81 = (bf16[4,96,512]{2,1,0:T(8,128)(2,1)S(1)}, f32[4,96,512]{2,1,0:T(8,128)S(1)}) custom-call(s32[1]{0:T(128)} %bitcast.me_ref.refs_0_, bf16[256,384]{1,0:T(8,128)(2,1)S(1)} %bitcast.12, bf16[8,48,2048]{2,1,0:T(8,128)(2,1)S(1)} %collective-permute-done.refs_0_.refs_2_, bf16[8,48,2048]{2,1,0:T(8,128)(2,1)} %collective-permute-done.1.refs_1_.refs_3_, ...), custom_call_target="tpu_custom_call" | custom-call | flops 1610612736 | bytes 4325376 | tf_op jit(solution)/shard_map/pallas_call | solution.py:417
  45.5 1.9 %collective-permute-start.9 = (bf16[2,96,256]{2,1,0:T(8,128)(2,1)S(1)}, bf16[2,96,256]{2,1,0:T(8,128)(2,1)S(1)}, u32[]{:S(2)}, u32[]{:S(2)}) collective-permute-start(bf16[2,96,256]{2,1,0:T(8,128)(2,1)S(1)} %add_convert_fusion.5), channel_id=1, source_target_pairs={{0,8},{1,9},{2,10},{3,11},{4,12},{5,13},{6,14},{7,15},{8,0},{9,1},... | collective-permute-start | bytes 294920 | tf_op jit(solution)/shard_map/ppermute | solution.py:315
  47.5 5.6 %shard_map.86 = (bf16[4,96,512]{2,1,0:T(8,128)(2,1)S(1)}, f32[4,96,512]{2,1,0:T(8,128)S(1)}) custom-call(s32[1]{0:T(128)} %bitcast.me_ref.refs_0_, bf16[256,384]{1,0:T(8,128)(2,1)S(1)} %bitcast.13, bf16[8,48,2048]{2,1,0:T(8,128)(2,1)S(1)} %copy-done.4, bf16[8,48,2048]{2,1,0:T(8,128)(2,1)S(1)} %copy-done.6, ...), custom_call_target="tpu_custom_call" | custom-call | flops 3221225472 | bytes 7471104 | tf_op jit(solution)/shard_map/pallas_call | solution.py:417
  55.5 2.1 %collective-permute-start.3 = (bf16[2,96,512]{2,1,0:T(8,128)(2,1)S(1)}, bf16[2,96,512]{2,1,0:T(8,128)(2,1)S(1)}, u32[]{:S(2)}, u32[]{:S(2)}) collective-permute-start(bf16[2,96,512]{2,1,0:T(8,128)(2,1)S(1)} %add_convert_fusion.2), channel_id=1, source_target_pairs={{0,4},{1,5},{2,6},{3,7},{4,0},{5,1},{6,2},{7,3},{8,12},{9,13},{10,... | collective-permute-start | bytes 589832 | tf_op jit(solution)/shard_map/ppermute | solution.py:315
  57.6 18.6 %collective-permute-done.11.refs_7_ = bf16[4,96,512]{2,1,0:T(8,128)(2,1)S(1)} collective-permute-done((bf16[4,96,512]{2,1,0:T(8,128)(2,1)S(1)}, bf16[4,96,512]{2,1,0:T(8,128)(2,1)S(1)}, u32[]{:S(2)}, u32[]{:S(2)}) %collective-permute-start.11) | collective-permute-done | bytes 393248 | tf_op jit(solution)/shard_map/ppermute | solution.py:315
  78.5 1.7 %collective-permute-start.4 = (bf16[1,96,512]{2,1,0:T(8,128)(2,1)S(1)}, bf16[1,96,512]{2,1,0:T(8,128)(2,1)S(1)}, u32[]{:S(2)}, u32[]{:S(2)}) collective-permute-start(bf16[1,96,512]{2,1,0:T(8,128)(2,1)S(1)} %add_convert_fusion.6), channel_id=1, source_target_pairs={{0,8},{1,9},{2,10},{3,11},{4,12},{5,13},{6,14},{7,15},{8,0},{9,1},... | collective-permute-start | bytes 294920 | tf_op jit(solution)/shard_map/ppermute | solution.py:315
  80.2 7.1 %collective-permute-done.12.refs_8_ = bf16[2,96,512]{2,1,0:T(8,128)(2,1)S(1)} collective-permute-done((bf16[2,96,512]{2,1,0:T(8,128)(2,1)S(1)}, bf16[2,96,512]{2,1,0:T(8,128)(2,1)S(1)}, u32[]{:S(2)}, u32[]{:S(2)}) %collective-permute-start.12) | collective-permute-done | bytes 196640 | tf_op jit(solution)/shard_map/ppermute | solution.py:315
  87.4 4.0 %collective-permute-done.6.refs_6_ = bf16[2,96,768]{2,1,0:T(8,128)(2,1)S(1)} collective-permute-done((bf16[2,96,768]{2,1,0:T(8,128)(2,1)S(1)}, bf16[2,96,768]{2,1,0:T(8,128)(2,1)S(1)}, u32[]{:S(2)}, u32[]{:S(2)}) %collective-permute-start.6) | collective-permute-done | bytes 294944 | tf_op jit(solution)/shard_map/ppermute | solution.py:315
  91.8 8.7 %collective-permute-done.7.refs_7_ = bf16[1,96,768]{2,1,0:T(8,128)(2,1)S(1)} collective-permute-done((bf16[1,96,768]{2,1,0:T(8,128)(2,1)S(1)}, bf16[1,96,768]{2,1,0:T(8,128)(2,1)S(1)}, u32[]{:S(2)}, u32[]{:S(2)}) %collective-permute-start.7) | collective-permute-done | bytes 147488 | tf_op jit(solution)/shard_map/ppermute | solution.py:315
  102.4 2.7 %shard_map.87 = (f32[8,288,128]{2,1,0:T(8,128)S(1)}, f32[8,288,128]{2,1,0:T(8,128)S(1)}) custom-call(s32[1]{0:T(128)} %bitcast.me_ref.refs_0_, s32[16]{0:T(128)S(1)} %copy-done.3, bf16[256,384]{1,0:T(8,128)(2,1)S(1)} %bitcast.15, bf16[48,16,256]{2,1,0:T(8,128)(2,1)S(1)} %shard_map.83.refs_3_, bf16[768,2048]{1,0:T(8,128)(2,1)S(1)} %bitcast.9, ...), custom_call_target="tpu_custom_call" | custom-call | tf_op jit(solution)/shard_map/pallas_call | solution.py:477
  105.2 2.8 %collective-permute-done.14.refs_1_ = f32[8,288,128]{2,1,0:T(8,128)S(1)} collective-permute-done((f32[8,288,128]{2,1,0:T(8,128)S(1)}, f32[8,288,128]{2,1,0:T(8,128)S(1)}, u32[]{:S(2)}, u32[]{:S(2)}) %collective-permute-start.14) | collective-permute-done | bytes 1179680 | tf_op jit(solution)/shard_map/ppermute | solution.py:315
  109.8 4.4 %collective-permute-done.15.refs_2_ = bf16[4,144,128]{2,1,0:T(8,128)(2,1)S(1)} collective-permute-done((bf16[4,144,128]{2,1,0:T(8,128)(2,1)S(1)}, bf16[4,144,128]{2,1,0:T(8,128)(2,1)S(1)}, u32[]{:S(2)}, u32[]{:S(2)}) %collective-permute-start.15) | collective-permute-done | bytes 147488 | tf_op jit(solution)/shard_map/ppermute | solution.py:315
  115.8 1.6 %collective-permute-start.19 = (bf16[2,144,128]{2,1,0:T(8,128)(2,1)S(1)}, bf16[2,144,128]{2,1,0:T(8,128)(2,1)S(1)}, u32[]{:S(2)}, u32[]{:S(2)}) collective-permute-start(bf16[2,144,128]{2,1,0:T(8,128)(2,1)S(1)} %get-tuple-element.32), channel_id=1, source_target_pairs={{0,8},{1,9},{2,10},{3,11},{4,12},{5,13},{6,14},{7,15},{8,0},{9,1},... | collective-permute-start | bytes 221192 | tf_op jit(solution)/shard_map/ppermute | solution.py:315
  117.5 2.4 %collective-permute-done.16.refs_3_ = bf16[2,144,128]{2,1,0:T(8,128)(2,1)S(1)} collective-permute-done((bf16[2,144,128]{2,1,0:T(8,128)(2,1)S(1)}, bf16[2,144,128]{2,1,0:T(8,128)(2,1)S(1)}, u32[]{:S(2)}, u32[]{:S(2)}) %collective-permute-start.16) | collective-permute-done | bytes 73760 | tf_op jit(solution)/shard_map/ppermute | solution.py:315
  121.2 1.7 %collective-permute-start.17 = (bf16[1,144,128]{2,1,0:T(8,128)(2,1)S(1)}, bf16[1,144,128]{2,1,0:T(8,128)(2,1)S(1)}, u32[]{:S(2)}, u32[]{:S(2)}) collective-permute-start(bf16[1,144,128]{2,1,0:T(8,128)(2,1)S(1)} %get-tuple-element.31), channel_id=1, source_target_pairs={{0,8},{1,9},{2,10},{3,11},{4,12},{5,13},{6,14},{7,15},{8,0},{9,1},... | collective-permute-start | bytes 110600 | tf_op jit(solution)/shard_map/ppermute | solution.py:315
  123.8 2.3 %collective-permute-done.17.refs_4_ = bf16[1,144,128]{2,1,0:T(8,128)(2,1)S(1)} collective-permute-done((bf16[1,144,128]{2,1,0:T(8,128)(2,1)S(1)}, bf16[1,144,128]{2,1,0:T(8,128)(2,1)S(1)}, u32[]{:S(2)}, u32[]{:S(2)}) %collective-permute-start.17) | collective-permute-done | bytes 36896 | tf_op jit(solution)/shard_map/ppermute | solution.py:315
  (62 shorter events, 21.4 us)
Async XLA Ops:
  4.4 22.3 %collective-permute-start = (bf16[8,48,2048]{2,1,0:T(8,128)(2,1)}, bf16[8,48,2048]{2,1,0:T(8,128)(2,1)S(1)}, u32[]{:S(2)}, u32[]{:S(2)}) collective-permute-start(bf16[8,48,2048]{2,1,0:T(8,128)(2,1)} %get-tuple-element.16), channel_id=1, source_target_pairs={{0,1},{1,0},{2,3},{3,2},{4,5},{5,4},{6,7},{7,6},{8,9},{9,8},{10,11... | collective-permute-start | bytes 4718600 | tf_op jit(solution)/shard_map/ppermute | solution.py:396
  8.8 18.0 %collective-permute-start.1 = (bf16[8,48,2048]{2,1,0:T(8,128)(2,1)}, bf16[8,48,2048]{2,1,0:T(8,128)(2,1)}, u32[]{:S(2)}, u32[]{:S(2)}) collective-permute-start(bf16[8,48,2048]{2,1,0:T(8,128)(2,1)} %get-tuple-element.17), channel_id=1, source_target_pairs={{0,1},{1,0},{2,3},{3,2},{4,5},{5,4},{6,7},{7,6},{8,9},{9,8},{10,11... | collective-permute-start | bytes 4718600 | tf_op jit(solution)/shard_map/ppermute | solution.py:396
  10.4 16.4 %all-to-all-start = ((bf16[16,16,384]{2,1,0:T(8,128)(2,1)}), bf16[16,16,384]{2,1,0:T(8,128)(2,1)S(1)}, u32[]{:S(2)}, u32[]{:S(2)}) async-start(bf16[16,16,384]{2,1,0:T(8,128)(2,1)} %shard_map.77), calls=%async_computation | async-start | bytes 393216 | tf_op jit(solution)/shard_map/all_to_all | solution.py:370
  37.2 8.3 %collective-permute-start.8 = (bf16[4,96,256]{2,1,0:T(8,128)(2,1)S(1)}, bf16[4,96,256]{2,1,0:T(8,128)(2,1)S(1)}, u32[]{:S(2)}, u32[]{:S(2)}) collective-permute-start(bf16[4,96,256]{2,1,0:T(8,128)(2,1)S(1)} %get-tuple-element.25), channel_id=1, source_target_pairs={{0,4},{1,5},{2,6},{3,7},{4,0},{5,1},{6,2},{7,3},{8,12},{9,13},{10,... | collective-permute-start | bytes 589832 | tf_op jit(solution)/shard_map/ppermute | solution.py:315
  39.4 8.1 %copy-start.6 = (bf16[8,48,2048]{2,1,0:T(8,128)(2,1)S(1)}, bf16[8,48,2048]{2,1,0:T(8,128)(2,1)}, u32[]{:S(2)}) copy-start(bf16[8,48,2048]{2,1,0:T(8,128)(2,1)} %get-tuple-element.19.refs_1_) | copy-start | bytes 4718596
  43.4 12.1 %collective-permute-start.2 = (bf16[4,96,512]{2,1,0:T(8,128)(2,1)S(1)}, bf16[4,96,512]{2,1,0:T(8,128)(2,1)S(1)}, u32[]{:S(2)}, u32[]{:S(2)}) collective-permute-start(bf16[4,96,512]{2,1,0:T(8,128)(2,1)S(1)} %get-tuple-element.21), channel_id=1, source_target_pairs={{0,2},{1,3},{2,0},{3,1},{4,6},{5,7},{6,4},{7,5},{8,10},{9,11},{10,... | collective-permute-start | bytes 1179656 | tf_op jit(solution)/shard_map/ppermute | solution.py:315
  44.4 33.2 %collective-permute-start.5 = (bf16[4,96,768]{2,1,0:T(8,128)(2,1)S(1)}, bf16[4,96,768]{2,1,0:T(8,128)(2,1)S(1)}, u32[]{:S(2)}, u32[]{:S(2)}) collective-permute-start(bf16[4,96,768]{2,1,0:T(8,128)(2,1)S(1)} %get-tuple-element.23), channel_id=1, source_target_pairs={{0,2},{1,3},{2,0},{3,1},{4,6},{5,7},{6,4},{7,5},{8,10},{9,11},{10,... | collective-permute-start | bytes 1769480 | tf_op jit(solution)/shard_map/ppermute | solution.py:315
  45.5 9.1 %collective-permute-start.9 = (bf16[2,96,256]{2,1,0:T(8,128)(2,1)S(1)}, bf16[2,96,256]{2,1,0:T(8,128)(2,1)S(1)}, u32[]{:S(2)}, u32[]{:S(2)}) collective-permute-start(bf16[2,96,256]{2,1,0:T(8,128)(2,1)S(1)} %add_convert_fusion.5), channel_id=1, source_target_pairs={{0,8},{1,9},{2,10},{3,11},{4,12},{5,13},{6,14},{7,15},{8,0},{9,1},... | collective-permute-start | bytes 294920 | tf_op jit(solution)/shard_map/ppermute | solution.py:315
  53.0 23.2 %collective-permute-start.11 = (bf16[4,96,512]{2,1,0:T(8,128)(2,1)S(1)}, bf16[4,96,512]{2,1,0:T(8,128)(2,1)S(1)}, u32[]{:S(2)}, u32[]{:S(2)}) collective-permute-start(bf16[4,96,512]{2,1,0:T(8,128)(2,1)S(1)} %get-tuple-element.27), channel_id=1, source_target_pairs={{0,2},{1,3},{2,0},{3,1},{4,6},{5,7},{6,4},{7,5},{8,10},{9,11},{10,... | collective-permute-start | bytes 1179656 | tf_op jit(solution)/shard_map/ppermute | solution.py:315
  54.6 37.2 %collective-permute-start.10 = (bf16[1,96,256]{2,1,0:T(8,128)(2,1)S(1)}, bf16[1,96,256]{2,1,0:T(8,128)(2,1)S(1)}, u32[]{:S(2)}, u32[]{:S(2)}) collective-permute-start(bf16[1,96,256]{2,1,0:T(8,128)(2,1)S(1)} %add_convert_fusion.7), channel_id=1, source_target_pairs={{0,2},{1,3},{2,0},{3,1},{4,6},{5,7},{6,4},{7,5},{8,10},{9,11},{10,... | collective-permute-start | bytes 147464 | tf_op jit(solution)/shard_map/ppermute | solution.py:315
  55.5 23.0 %collective-permute-start.3 = (bf16[2,96,512]{2,1,0:T(8,128)(2,1)S(1)}, bf16[2,96,512]{2,1,0:T(8,128)(2,1)S(1)}, u32[]{:S(2)}, u32[]{:S(2)}) collective-permute-start(bf16[2,96,512]{2,1,0:T(8,128)(2,1)S(1)} %add_convert_fusion.2), channel_id=1, source_target_pairs={{0,4},{1,5},{2,6},{3,7},{4,0},{5,1},{6,2},{7,3},{8,12},{9,13},{10,... | collective-permute-start | bytes 589832 | tf_op jit(solution)/shard_map/ppermute | solution.py:315
  76.2 11.0 %collective-permute-start.12 = (bf16[2,96,512]{2,1,0:T(8,128)(2,1)S(1)}, bf16[2,96,512]{2,1,0:T(8,128)(2,1)S(1)}, u32[]{:S(2)}, u32[]{:S(2)}) collective-permute-start(bf16[2,96,512]{2,1,0:T(8,128)(2,1)S(1)} %add_convert_fusion.1), channel_id=1, source_target_pairs={{0,4},{1,5},{2,6},{3,7},{4,0},{5,1},{6,2},{7,3},{8,12},{9,13},{10,... | collective-permute-start | bytes 589832 | tf_op jit(solution)/shard_map/ppermute | solution.py:315
  77.7 13.6 %collective-permute-start.6 = (bf16[2,96,768]{2,1,0:T(8,128)(2,1)S(1)}, bf16[2,96,768]{2,1,0:T(8,128)(2,1)S(1)}, u32[]{:S(2)}, u32[]{:S(2)}) collective-permute-start(bf16[2,96,768]{2,1,0:T(8,128)(2,1)S(1)} %add_convert_fusion), channel_id=1, source_target_pairs={{0,4},{1,5},{2,6},{3,7},{4,0},{5,1},{6,2},{7,3},{8,12},{9,13},{10,... | collective-permute-start | bytes 884744 | tf_op jit(solution)/shard_map/ppermute | solution.py:315
  78.5 13.3 %collective-permute-start.4 = (bf16[1,96,512]{2,1,0:T(8,128)(2,1)S(1)}, bf16[1,96,512]{2,1,0:T(8,128)(2,1)S(1)}, u32[]{:S(2)}, u32[]{:S(2)}) collective-permute-start(bf16[1,96,512]{2,1,0:T(8,128)(2,1)S(1)} %add_convert_fusion.6), channel_id=1, source_target_pairs={{0,8},{1,9},{2,10},{3,11},{4,12},{5,13},{6,14},{7,15},{8,0},{9,1},... | collective-permute-start | bytes 294920 | tf_op jit(solution)/shard_map/ppermute | solution.py:315
  87.3 14.2 %collective-permute-start.13 = (bf16[1,96,512]{2,1,0:T(8,128)(2,1)S(1)}, bf16[1,96,512]{2,1,0:T(8,128)(2,1)S(1)}, u32[]{:S(2)}, u32[]{:S(2)}) collective-permute-start(bf16[1,96,512]{2,1,0:T(8,128)(2,1)S(1)} %add_convert_fusion.4), channel_id=1, source_target_pairs={{0,8},{1,9},{2,10},{3,11},{4,12},{5,13},{6,14},{7,15},{8,0},{9,1},... | collective-permute-start | bytes 294920 | tf_op jit(solution)/shard_map/ppermute | solution.py:315
  91.4 9.1 %collective-permute-start.7 = (bf16[1,96,768]{2,1,0:T(8,128)(2,1)S(1)}, bf16[1,96,768]{2,1,0:T(8,128)(2,1)S(1)}, u32[]{:S(2)}, u32[]{:S(2)}) collective-permute-start(bf16[1,96,768]{2,1,0:T(8,128)(2,1)S(1)} %add_convert_fusion.3), channel_id=1, source_target_pairs={{0,8},{1,9},{2,10},{3,11},{4,12},{5,13},{6,14},{7,15},{8,0},{9,1},... | collective-permute-start | bytes 442376 | tf_op jit(solution)/shard_map/ppermute | solution.py:315
  91.8 9.7 %copy-start.3 = (s32[16]{0:T(128)S(1)}, s32[16]{0:T(128)}, u32[]{:S(2)}) copy-start(s32[16]{0:T(128)} %refs_1_.1) | copy-start | bytes 196
  105.1 2.9 %collective-permute-start.14 = (f32[8,288,128]{2,1,0:T(8,128)S(1)}, f32[8,288,128]{2,1,0:T(8,128)S(1)}, u32[]{:S(2)}, u32[]{:S(2)}) collective-permute-start(f32[8,288,128]{2,1,0:T(8,128)S(1)} %get-tuple-element.29), channel_id=1, source_target_pairs={{0,1},{1,0},{2,3},{3,2},{4,5},{5,4},{6,7},{7,6},{8,9},{9,8},{10,11... | collective-permute-start | bytes 3538952 | tf_op jit(solution)/shard_map/ppermute | solution.py:315
  108.2 6.0 %collective-permute-start.15 = (bf16[4,144,128]{2,1,0:T(8,128)(2,1)S(1)}, bf16[4,144,128]{2,1,0:T(8,128)(2,1)S(1)}, u32[]{:S(2)}, u32[]{:S(2)}) collective-permute-start(bf16[4,144,128]{2,1,0:T(8,128)(2,1)S(1)} %get-tuple-element.35), channel_id=1, source_target_pairs={{0,2},{1,3},{2,0},{3,1},{4,6},{5,7},{6,4},{7,5},{8,10},{9,11},{10,... | collective-permute-start | bytes 442376 | tf_op jit(solution)/shard_map/ppermute | solution.py:315
  109.8 5.6 %collective-permute-start.18 = (bf16[4,144,128]{2,1,0:T(8,128)(2,1)S(1)}, bf16[4,144,128]{2,1,0:T(8,128)(2,1)S(1)}, u32[]{:S(2)}, u32[]{:S(2)}) collective-permute-start(bf16[4,144,128]{2,1,0:T(8,128)(2,1)S(1)} %get-tuple-element.34), channel_id=1, source_target_pairs={{0,4},{1,5},{2,6},{3,7},{4,0},{5,1},{6,2},{7,3},{8,12},{9,13},{10,... | collective-permute-start | bytes 442376 | tf_op jit(solution)/shard_map/ppermute | solution.py:315
  115.5 4.4 %collective-permute-start.16 = (bf16[2,144,128]{2,1,0:T(8,128)(2,1)S(1)}, bf16[2,144,128]{2,1,0:T(8,128)(2,1)S(1)}, u32[]{:S(2)}, u32[]{:S(2)}) collective-permute-start(bf16[2,144,128]{2,1,0:T(8,128)(2,1)S(1)} %get-tuple-element.33), channel_id=1, source_target_pairs={{0,4},{1,5},{2,6},{3,7},{4,0},{5,1},{6,2},{7,3},{8,12},{9,13},{10,... | collective-permute-start | bytes 221192 | tf_op jit(solution)/shard_map/ppermute | solution.py:315
  115.8 5.3 %collective-permute-start.19 = (bf16[2,144,128]{2,1,0:T(8,128)(2,1)S(1)}, bf16[2,144,128]{2,1,0:T(8,128)(2,1)S(1)}, u32[]{:S(2)}, u32[]{:S(2)}) collective-permute-start(bf16[2,144,128]{2,1,0:T(8,128)(2,1)S(1)} %get-tuple-element.32), channel_id=1, source_target_pairs={{0,8},{1,9},{2,10},{3,11},{4,12},{5,13},{6,14},{7,15},{8,0},{9,1},... | collective-permute-start | bytes 221192 | tf_op jit(solution)/shard_map/ppermute | solution.py:315
  121.2 4.9 %collective-permute-start.17 = (bf16[1,144,128]{2,1,0:T(8,128)(2,1)S(1)}, bf16[1,144,128]{2,1,0:T(8,128)(2,1)S(1)}, u32[]{:S(2)}, u32[]{:S(2)}) collective-permute-start(bf16[1,144,128]{2,1,0:T(8,128)(2,1)S(1)} %get-tuple-element.31), channel_id=1, source_target_pairs={{0,8},{1,9},{2,10},{3,11},{4,12},{5,13},{6,14},{7,15},{8,0},{9,1},... | collective-permute-start | bytes 110600 | tf_op jit(solution)/shard_map/ppermute | solution.py:315
  122.9 4.0 %collective-permute-start.20 = (bf16[1,144,128]{2,1,0:T(8,128)(2,1)S(1)}, bf16[1,144,128]{2,1,0:T(8,128)(2,1)S(1)}, u32[]{:S(2)}, u32[]{:S(2)}) collective-permute-start(bf16[1,144,128]{2,1,0:T(8,128)(2,1)S(1)} %get-tuple-element.30), channel_id=1, source_target_pairs={{0,2},{1,3},{2,0},{3,1},{4,6},{5,7},{6,4},{7,5},{8,10},{9,11},{10,... | collective-permute-start | bytes 110600 | tf_op jit(solution)/shard_map/ppermute | solution.py:315
  (5 other events, 11.8 us)
